TPU v7x, 128 devices: a whole 4x4x4 slice. The times are simulated.
128 devices in a mesh: seq: 32 (over z, x, core), ch: 4 (over y).
Axes of the slice: x: 4, y: 4, z: 4, core: 2. Of those that a mesh axis runs over, the one named last changes fastest.
Arguments:
- inputs: float32 [8192, 4096], P('seq', 'ch'), may hold values from -6 to 6
- out_grads: float32 [8192, 4096], P('seq', 'ch'), may hold values from -0.12 to 0.12
- tile_order: int32 [32], replicated, may hold values from 0 to 31, each once
- lag_order: int32 [32], replicated, may hold values from 0 to 31, each once
Outputs:
- filter_grad: float32 [256, 8192], P('ch', 'seq')
Inputs may be any that keep to these rules, and one draw needn't show every extreme that they name: Row block i of inputs and out_grads holds sequence tile tile_order[i]; every tile appears once. Column block i of filter_grad holds lag block lag_order[i]; every lag block appears once.
All inputs are finite; a program needn't handle non-finite values.
Results may differ from a plain program's by a relative error of at most 0.000098.
Values sent between devices are 32-bit elements; how exact they have to be, the bound alone decides.
A program may use at most 128 MiB of HBM per device.

v0:
```python
import math

import jax
import jax.numpy as jnp
from jax import lax
from jax.sharding import PartitionSpec as P

C = 4096
GROUP = 16


target_ratio = 0.5
epsilon = 1e-12
highest = lax.Precision.HIGHEST


def forward_table(tile_rows):
    double_rows = 2 * tile_rows
    frequency = lax.iota(jnp.int32, tile_rows + 1)[:, None]
    places = lax.iota(jnp.int32, tile_rows)[None, :]
    angles = (frequency * places % double_rows).astype(jnp.float32) * (math.pi / tile_rows)
    cosine_rows = jnp.cos(angles)
    sine_rows = -jnp.sin(angles[1:tile_rows])
    return jnp.concatenate([cosine_rows, sine_rows], axis=0)


def inverse_table(tile_rows):
    double_rows = 2 * tile_rows
    frequency = lax.iota(jnp.int32, tile_rows + 1)[:, None]
    lag_index = lax.iota(jnp.int32, double_rows)[None, :]
    angles = (frequency * lag_index % double_rows).astype(jnp.float32) * (math.pi / tile_rows)
    weights = jnp.where((frequency == 0) | (frequency == tile_rows), 1.0, 2.0).astype(jnp.float32)
    cosine_rows = weights * jnp.cos(angles) / double_rows
    sine_rows = -2.0 * jnp.sin(angles[1:tile_rows]) / double_rows
    return jnp.concatenate([cosine_rows, sine_rows], axis=0)


def spectrum(transform, values):
    return jnp.dot(transform, values, precision=highest, preferred_element_type=jnp.float32)


def lag_terms(input_spec, grad_spec, inverse, tile_rows):
    input_real = input_spec[: tile_rows + 1]
    input_imag = input_spec[tile_rows + 1 :]
    grad_real = grad_spec[: tile_rows + 1]
    grad_imag = grad_spec[tile_rows + 1 :]
    real_part = input_real * grad_real + jnp.pad(input_imag * grad_imag, ((1, 1), (0, 0)))
    imag_part = grad_imag * input_real[1:tile_rows] - grad_real[1:tile_rows] * input_imag
    packed = jnp.concatenate([real_part, imag_part], axis=0)
    grouped = packed.reshape(packed.shape[0], packed.shape[1] // GROUP, GROUP).sum(axis=2)
    return jnp.dot(grouped.T, inverse, precision=highest, preferred_element_type=jnp.float32)


def add_pair(carried, lag_values, offset, weight, tile_rows):
    blocks = carried.shape[1] // tile_rows
    usable = weight * (offset >= 0).astype(jnp.float32)
    lower_part = lag_values[:, :tile_rows] * usable
    upper_part = lag_values[:, tile_rows:] * (usable * (offset >= 1).astype(jnp.float32))
    lower_start = jnp.clip(offset, 0, blocks - 1) * tile_rows
    carried = lax.dynamic_update_slice_in_dim(
        carried,
        lax.dynamic_slice_in_dim(carried, lower_start, tile_rows, 1) + lower_part,
        lower_start,
        1,
    )
    high_start = jnp.clip(offset - 1, 0, blocks - 1) * tile_rows
    carried = lax.dynamic_update_slice_in_dim(
        carried,
        lax.dynamic_slice_in_dim(carried, high_start, tile_rows, 1) + upper_part,
        high_start,
        1,
    )
    return carried


def shards(inputs, out_grads, tile_order, lag_order):
    tile_rows = inputs.shape[0]
    seq_devices = lax.axis_size("seq")
    lag_total = tile_rows * seq_devices
    groups_here = inputs.shape[1] // GROUP
    forward = forward_table(tile_rows)
    inverse = inverse_table(tile_rows)
    position = lax.axis_index("seq")
    own_tile = lax.dynamic_index_in_dim(tile_order, position, keepdims=False)
    own_grads = spectrum(forward, out_grads)
    zeroed = jnp.zeros((groups_here, lag_total), jnp.float32)

    def absorb(carried, spectrum_part, source_device):
        source_tile = lax.dynamic_index_in_dim(tile_order, source_device, keepdims=False)
        return add_pair(
            carried,
            lag_terms(spectrum_part, own_grads, inverse, tile_rows),
            own_tile - source_tile,
            1.0,
            tile_rows,
        )

    pieces = lax.all_gather(inputs, "seq", axis=0, tiled=True)
    count_rows = pieces.shape[0]
    stacked = pieces.reshape(count_rows // tile_rows, tile_rows, pieces.shape[1])

    def visit_tile(running, packet):
        tile_block, number = packet
        return (absorb(running, spectrum(forward, tile_block), number), None)

    carried = lax.scan(visit_tile, zeroed, (stacked, lax.iota(jnp.int32, count_rows // tile_rows)))[
        0
    ]
    reordered = carried.reshape(groups_here, seq_devices, tile_rows)[:, lag_order].reshape(
        groups_here, lag_total
    )
    owned = lax.psum_scatter(reordered, "seq", scatter_dimension=1, tiled=True)
    squares = lax.psum(jnp.sum(owned * owned), ("seq", "ch"))
    total_entries = C // GROUP * lag_total
    factor = target_ratio * math.sqrt(total_entries) / jnp.sqrt(squares + epsilon)
    return owned * factor


def solution(mesh):
    return jax.shard_map(
        shards,
        mesh=mesh,
        in_specs=(P("seq", "ch"), P("seq", "ch"), P(), P()),
        out_specs=P("ch", "seq"),
        check_vma=False,
    )
```

profile of v0, /device:TPU:1, one launch (start us, length us, event | category | flops | bytes accessed | tf_op | source)
XLA Modules:
  0.0 856.6 jit_solution(5725800268494179742)
XLA Ops:
  18.6 108.5 %all-gather.2.cloned.1.call-done = f32[8192,1024]{1,0:T(8,128)} async-done(((f32[256,1024]{1,0:T(8,128)}), f32[8192,1024]{1,0:T(8,128)}) %all-gather.2.cloned.1.call-update) | async-done | bytes 33554448 | tf_op jit(solution)/shard_map/all_gather | solution.py:98
  128.6 568.1 %while.12 = (s32[]{:T(128)}, f32[64,8192]{1,0:T(8,128)}, s32[32]{0:T(128)S(1)}, s32[32]{0:T(128)S(1)}, s32[]{:T(128)}, /*index=5*/f32[32,256,1024]{2,1,0:T(8,128...) while((s32[]{:T(128)}, f32[64,8192]{1,0:T(8,128)}, ...), condition=%wide.region_2.3_spmd, body=%wide.region_0.2_spmd.sunk | while | flops 1814591488 | bytes 43237868 | solution.py:106
  133.1 3.2 convolution_bitcast_fusion.2
  150.8 3.2 convolution_bitcast_fusion.2
  168.6 3.2 convolution_bitcast_fusion.2
  174.7 2.2 bitcast_reduce_fusion.2
  186.3 3.2 convolution_bitcast_fusion.2
  192.5 2.2 bitcast_reduce_fusion.2
  204.1 3.2 convolution_bitcast_fusion.2
  210.3 2.2 bitcast_reduce_fusion.2
  221.9 3.2 convolution_bitcast_fusion.2
  239.7 3.2 convolution_bitcast_fusion.2
  245.8 2.2 bitcast_reduce_fusion.2
  257.4 3.2 convolution_bitcast_fusion.2
  263.5 2.2 bitcast_reduce_fusion.2
  275.2 3.2 convolution_bitcast_fusion.2
  281.3 2.2 bitcast_reduce_fusion.2
  292.9 3.2 convolution_bitcast_fusion.2
  299.1 2.2 bitcast_reduce_fusion.2
  310.7 3.2 convolution_bitcast_fusion.2
  316.8 2.2 bitcast_reduce_fusion.2
  328.4 3.2 convolution_bitcast_fusion.2
  334.6 2.2 bitcast_reduce_fusion.2
  346.2 3.2 convolution_bitcast_fusion.2
  352.3 2.2 bitcast_reduce_fusion.2
  363.9 3.2 convolution_bitcast_fusion.2
  381.7 3.2 convolution_bitcast_fusion.2
  399.4 3.2 convolution_bitcast_fusion.2
  417.2 3.2 convolution_bitcast_fusion.2
  434.9 3.2 convolution_bitcast_fusion.2
  452.7 3.2 convolution_bitcast_fusion.2
  470.4 3.2 convolution_bitcast_fusion.2
  476.6 2.2 bitcast_reduce_fusion.2
  488.2 3.2 convolution_bitcast_fusion.2
  506.0 3.2 convolution_bitcast_fusion.2
  523.7 3.2 convolution_bitcast_fusion.2
  541.5 3.2 convolution_bitcast_fusion.2
  559.2 3.2 convolution_bitcast_fusion.2
  576.9 3.2 convolution_bitcast_fusion.2
  594.7 3.2 convolution_bitcast_fusion.2
  612.5 3.2 convolution_bitcast_fusion.2
  630.2 3.2 convolution_bitcast_fusion.2
  647.9 3.2 convolution_bitcast_fusion.2
  665.7 3.2 convolution_bitcast_fusion.2
  683.4 3.2 convolution_bitcast_fusion.2
  700.6 3.1 copy.13
  703.7 76.4 %reduce-scatter.2.cloned.1.call-done = f32[64,256]{1,0:T(8,128)} async-done(((f32[64,8192]{1,0:T(8,128)}), f32[64,256]{1,0:T(8,128)}) %reduce-scatter.2.cloned.1.call-update) | async-done | bytes 65552 | tf_op jit(solution)/shard_map/reduce_scatter | solution.py:112
  781.6 66.0 %psum.7 = f32[]{:T(128)} all-reduce(f32[]{:T(128)} %multiply_reduce_fusion), channel_id=1, replica_groups=mesh['seq'=32,'ch'=4] {'seq','ch'}, use_global_device_ids=true, to_apply=%region_5.6 | all-reduce | flops 1 | bytes 8 | tf_op jit(solution)/shard_map/psum | solution.py:113
  (466 shorter events, 357.9 us)
Async XLA Ops:
  6.5 10.2 %copy-start = (f32[256,1024]{1,0:T(8,128)S(1)}, f32[256,1024]{1,0:T(8,128)}, u32[]{:S(2)}) copy-start(f32[256,1024]{1,0:T(8,128)} %param.7) | copy-start | bytes 3145732
  6.5 120.5 %all-gather.2.cloned.1.call-start = ((), (), s32[]{:S(2)}) async-start(), calls=%async_computation.1 | async-start | bytes 34603008 | tf_op jit(solution)/shard_map/all_gather | solution.py:98
  7.3 772.9 %reduce-scatter.2.cloned.1.call-start = ((), (), s32[]{:S(2)}) async-start(), calls=%async_computation.2 | async-start | bytes 2162688 | tf_op jit(solution)/shard_map/reduce_scatter | solution.py:112
  16.7 111.9 %copy-start.4 = (s32[32]{0:T(128)S(1)}, s32[32]{0:T(128)}, u32[]{:S(2)}) copy-start(s32[32]{0:T(128)} %param.8) | copy-start | bytes 388
  128.6 8.2 copy-start.1
  146.3 8.2 copy-start.1
  156.9 7.2 copy-start.2
  164.1 8.2 copy-start.1
  174.7 7.2 copy-start.2
  181.9 8.2 copy-start.1
  192.5 7.2 copy-start.2
  199.7 8.2 copy-start.1
  210.3 7.2 copy-start.2
  217.4 8.2 copy-start.1
  228.0 7.2 copy-start.2
  235.2 8.2 copy-start.1
  253.0 8.2 copy-start.1
  270.7 8.2 copy-start.1
  288.5 8.2 copy-start.1
  306.2 8.2 copy-start.1
  316.8 7.2 copy-start.2
  324.0 8.2 copy-start.1
  341.7 8.2 copy-start.1
  352.3 7.2 copy-start.2
  359.5 8.2 copy-start.1
  377.2 8.2 copy-start.1
  394.9 8.2 copy-start.1
  405.5 7.2 copy-start.2
  412.7 8.2 copy-start.1
  430.4 8.2 copy-start.1
  448.2 8.2 copy-start.1
  458.8 7.2 copy-start.2
  466.0 8.2 copy-start.1
  483.7 8.2 copy-start.1
  494.3 7.2 copy-start.2
  501.5 8.2 copy-start.1
  519.2 8.2 copy-start.1
  537.0 8.2 copy-start.1
  554.7 8.2 copy-start.1
  565.3 7.2 copy-start.2
  572.5 8.2 copy-start.1
  583.1 7.2 copy-start.2
  590.3 8.2 copy-start.1
  608.0 8.2 copy-start.1
  625.8 8.2 copy-start.1
  643.5 8.2 copy-start.1
  661.2 8.2 copy-start.1
  679.0 8.2 copy-start.1
  (21 other events, 148.6 us)
Sparse Core Ops, SparseCore 0:
  9.6 117.4 all-gather.1
  703.8 76.2 reduce-scatter.1
where the time goes:
time: 863 us; the launch traced here: 857 us
  other arithmetic  210 us (24%)
  waiting for transfers between devices  186 us (22%)
  matrix products  169 us (20%)
  local copies, waits for them, and re-layouts  110 us (13%)
  loops' own time  102 us (12%)
  blocking collectives  66 us (8%)
  between operations  14.2 us (2%)
    all_gather x1, waiting for transfers between devices, shards(): pieces = lax.all_gather(inputs, 'seq', axis=0, tiled=True)  109 us
    dot_general x33, matrix products, spectrum(): jnp.dot(transform, values, precision=highest, preferred_element_type=jnp....  106 us
    another operation x1, loops' own time, shards(): lax.scan(visit_tile, zeroed, (stacked, lax.iota(jnp.int32, count_rows //...  102 us
    dynamic_update_slice x64, other arithmetic, add_pair(): lax.dynamic_update_slice_in_dim(carried, lax.dynamic_slice_in_dim(carried...  95.5 us
    reduce_scatter x1, waiting for transfers between devices, shards(): owned = lax.psum_scatter(reordered, 'seq', scatter_dimension=1, tiled=True)  76.4 us
    reduce_sum x32, other arithmetic, lag_terms(): packed.reshape(packed.shape[0], packed.shape[1] // GROUP, GROUP).sum(axis=2)  70.5 us
    psum x1, blocking collectives, shards(): squares = lax.psum(jnp.sum(owned * owned), ('seq', 'ch'))  66 us
    dot_general x32, matrix products, lag_terms(): jnp.dot(grouped.T, inverse, precision=highest, preferred_element_type=jnp...  63 us
  transfers between devices with their start and end apart: 2, of which 2 were waited for; matrix products, arithmetic and copies ran while one was open for 1% of the time, Pallas kernels for 0%

commit v1 on v0

v1 whole, which is shorter than its diff:
```python
import functools
import math

import jax
import jax.numpy as jnp
import numpy as np
from jax import lax
from jax.experimental import pallas as pl
from jax.experimental.pallas import tpu as pltpu
from jax.sharding import PartitionSpec as P

C = 4096
GROUP = 16
target_ratio = 0.5
epsilon = 1e-12

MESH = pl.DeviceIdType.MESH
F32, BF16 = jnp.float32, jnp.bfloat16
SIDE = 4
POS = 16384
ROWS = 64
HOPS = (2, 1, 3, 0)
MOVES = tuple((d, k) for d in HOPS for k in (0, 1) if (d, k) != (0, 0))


def split(values):
    high = values.astype(BF16)
    return high, (values - high.astype(F32)).astype(BF16)


def dot3(left, right_high, right_low):
    high, low = split(left)
    dot = functools.partial(jnp.dot, preferred_element_type=F32)
    return dot(high, right_high) + (dot(low, right_high) + dot(high, right_low))


def tables():
    def halves(values):
        high = np.asarray(values, np.float32).astype(jnp.bfloat16)
        return high, (np.asarray(values, np.float32) - high.astype(np.float32)).astype(jnp.bfloat16)

    r = np.arange(128)
    angle = 2 * np.pi * (np.outer(r, r) % 128) / 128
    cos, sin = np.cos(angle), np.sin(angle)
    forward = np.block([[cos, -sin], [sin, cos]])
    inverse = np.block([[cos, sin], [-sin, cos]])
    m, n = np.divmod(np.arange(ROWS), 8)
    odd = 2 * (16 * n + m) + 1
    turn = np.pi * np.outer(odd, r) / POS
    twist = np.concatenate([np.cos(turn), np.sin(turn)], axis=1).astype(np.float32)
    step = 2 * np.arange(32)[None, :] + np.arange(2)[:, None]
    outer = np.pi * (np.outer(step.reshape(-1), odd) % 256) / 128
    ends = np.concatenate([np.cos(outer), -np.sin(outer)], axis=1) / (POS // 2)
    return halves(forward), halves(inverse), twist, halves(ends)


def place():
    me = lax.axis_index("seq")
    return me // 8, (me // 2) % 4, me % 2


def cmul(a, b, wr, wi):
    return a * wr - b * wi, a * wi + b * wr


def first_step(x):
    root = math.sqrt(0.5)
    s = [x[p + 4] * root for p in range(4)]
    plus = [x[p] + s[p] for p in range(4)]
    minus = [x[p] - s[p] for p in range(4)]
    out = [None] * 8
    for m in range(4):
        v = []
        for p in range(4):
            re = plus[p] if m in (0, 3) else minus[p]
            im = s[p]
            sign = -1.0 if m in (0, 1) else 1.0
            if p == 0:
                v.append((re, im if sign > 0 else -im))
            else:
                a = math.pi * (2 * m + 1) * p / 16
                wr, wi = math.cos(a), -math.sin(a)
                v.append((re * wr - im * (sign * wi), re * wi + im * (sign * wr)))
        e = (v[0][0] + v[2][0], v[0][1] + v[2][1])
        d = (v[0][0] - v[2][0], v[0][1] - v[2][1])
        f = (v[1][0] + v[3][0], v[1][1] + v[3][1])
        h = (v[1][0] - v[3][0], v[1][1] - v[3][1])
        out[m] = (e[0] + f[0], e[1] + f[1])
        out[m + 4] = (d[0] + h[1], d[1] - h[0])
    return out


def eight(z):
    add = lambda a, b: (a[0] + b[0], a[1] + b[1])
    sub = lambda a, b: (a[0] - b[0], a[1] - b[1])
    turn = lambda a: (a[1], -a[0])

    def four(a, b, c, d):
        e, f, g, h = add(a, c), sub(a, c), add(b, d), turn(sub(b, d))
        return add(e, g), add(f, h), sub(e, g), sub(f, h)

    even, odd = four(z[0], z[2], z[4], z[6]), four(z[1], z[3], z[5], z[7])
    root = math.sqrt(0.5)
    o1 = ((odd[1][0] + odd[1][1]) * root, (odd[1][1] - odd[1][0]) * root)
    o3 = ((odd[3][1] - odd[3][0]) * root, -(odd[3][0] + odd[3][1]) * root)
    turned = (odd[0], o1, turn(odd[2]), o3)
    return [add(even[k], turned[k]) for k in range(4)] + [sub(even[k], turned[k]) for k in range(4)]


def outer_steps(load, twist_ref, mid_ref, y_ref):
    def first(q2, carry):
        for half in range(2):
            out = first_step([load(4 * p + q2, half) for p in range(8)])
            for m in range(8):
                mid_ref[m, 2 * q2 + half, 0] = out[m][0]
                mid_ref[m, 2 * q2 + half, 1] = out[m][1]
        return carry

    lax.fori_loop(0, 4, first, 0)
    for m in range(8):
        z = []
        for q in range(8):
            re, im = mid_ref[m, q, 0], mid_ref[m, q, 1]
            a = math.pi * (2 * m + 1) * q / 128
            z.append((re, im) if q == 0 else cmul(re, im, math.cos(a), -math.sin(a)))
        for n, (re, im) in enumerate(eight(z)):
            row = 8 * m + n
            wr = twist_ref[pl.ds(row, 1), 0:128]
            wi = twist_ref[pl.ds(row, 1), 128:256]
            a, b = cmul(re, im, wr, -wi)
            y_ref[row, :, 0:128] = a
            y_ref[row, :, 128:256] = b


def transform(load, twist_ref, fh_ref, fl_ref, mid_ref, y_ref, spec_ref):
    outer_steps(load, twist_ref, mid_ref, y_ref)

    def rows(t, carry):
        at = pl.ds(t * 32, 32)
        spec_ref[at] = dot3(y_ref[at].reshape(256, 256), fh_ref[...], fl_ref[...]).reshape(32, 8, 256)
        return carry

    lax.fori_loop(0, ROWS // 32, rows, 0)


def multiply(u_ref, g_ref, acc_ref, fresh):
    def rows(t, carry):
        at = pl.ds(t * 4, 4)
        ur, ui = u_ref[at, :, 0:128], u_ref[at, :, 128:256]
        gr, gi = g_ref[at, :, 0:128], g_ref[at, :, 128:256]
        re, im = gr * ur + gi * ui, gi * ur - gr * ui
        if not fresh:
            re, im = re + acc_ref[at, :, 0:128], im + acc_ref[at, :, 128:256]
        acc_ref[at, :, 0:128] = re
        acc_ref[at, :, 128:256] = im
        return carry

    lax.fori_loop(0, ROWS // 4, rows, 0)


def to_lags(acc_ref, ih_ref, il_ref, twist_ref, eh_ref, el_ref):
    sums = jnp.sum(acc_ref[...], axis=1)
    v = dot3(sums, ih_ref[...], il_ref[...])
    re, im = cmul(v[:, 0:128], v[:, 128:256], twist_ref[:, 0:128], twist_ref[:, 128:256])
    high, low = split(jnp.concatenate([re, im], axis=0))
    dot = functools.partial(jnp.dot, preferred_element_type=F32)
    return dot(eh_ref[...], high) + (dot(eh_ref[...], low) + dot(el_ref[...], high))


def exchange_kernel(u_ref, g_ref, land, xin, turned, mid, insem, s_a, r_a, s_b, r_b, l_a, l_b):
    z, x, c = place()
    ch = lax.axis_index("ch")

    def device(kind, a, b, core):
        zz, xx = (b, a) if kind == 0 else (a, b)
        return (zz * 8 + xx * 2 + core, ch)

    mine = ((x, z), (z, x))
    incoming = []
    for step in HOPS:
        for kind in range(2):
            a = (mine[kind][0] + step) % SIDE
            for arr, ref in enumerate((u_ref, g_ref)):
                n = len(incoming)
                copy = pltpu.make_async_copy(
                    ref.at[:, pl.ds(pl.multiple_of(kind * 512 + a * 128, 128), 128)], xin.at[n], insem.at[n]
                )
                copy.start()
                incoming.append((copy, step, kind, a, arr))

    barrier = pltpu.get_barrier_semaphore()
    peers = [(kind, d, k) for kind in range(2) for d, k in MOVES if not (kind == 1 and d == 0)]
    for kind, d, k in peers:
        a, b = mine[kind]
        pl.semaphore_signal(barrier, inc=1, device_id=device(kind, (a + d) % SIDE, b, (c + k) % 2), device_id_type=MESH)
    pl.semaphore_wait(barrier, len(peers))

    def send_a(kind, kh, move):
        d, k = MOVES[move]
        a, b = mine[kind]
        to_a, to_c = (a + d) % SIDE, (c + k) % 2
        return pltpu.make_async_remote_copy(
            src_ref=turned.at[kind, to_a, to_c, :, kh],
            dst_ref=mid.at[kind, kh, :, a * 2 + c],
            send_sem=s_a.at[kind, kh, move],
            recv_sem=r_a.at[kind, kh, move],
            device_id=device(kind, to_a, b, to_c),
            device_id_type=MESH,
        )

    def own_a(kind, kh):
        a, _ = mine[kind]
        return pltpu.make_async_copy(turned.at[kind, a, c, :, kh], mid.at[kind, kh, :, a * 2 + c], l_a.at[kind, kh])

    def send_b(kind, kh, hop):
        a, b = mine[kind]
        to_b = (b + HOPS[hop]) % SIDE
        return pltpu.make_async_remote_copy(
            src_ref=mid.at[kind, kh, to_b],
            dst_ref=land.at[kind, kh, b],
            send_sem=s_b.at[kind, kh, hop],
            recv_sem=r_b.at[kind, kh, hop],
            device_id=device(kind, a, to_b, c),
            device_id_type=MESH,
        )

    def own_b(kind, kh):
        _, b = mine[kind]
        return pltpu.make_async_copy(mid.at[kind, kh, b], land.at[kind, kh, b], l_b.at[kind, kh])

    for n, (copy, step, kind, a, arr) in enumerate(incoming):
        copy.wait()
        turned[kind, a, :, :, :, arr] = xin[n].T.reshape(2, 4, 2, 8, 256)
        if arr == 1:
            for move, (d, k) in enumerate(MOVES):
                if d == step:
                    send_a(kind, 0, move).start()
            if step == 0:
                own_a(kind, 0).start()
    for kind in range(2):
        for move in range(len(MOVES)):
            send_a(kind, 1, move).start()
        own_a(kind, 1).start()
    for kh in range(2):
        for kind in range(2):
            own_a(kind, kh).wait()
            for move in range(len(MOVES)):
                send_a(kind, kh, move).wait_recv()
            for hop in range(3):
                send_b(kind, kh, hop).start()
            own_b(kind, kh).start()
    for kh in range(2):
        for kind in range(2):
            own_b(kind, kh).wait()
            for hop in range(3):
                send_b(kind, kh, hop).wait()
            for move in range(len(MOVES)):
                send_a(kind, kh, move).wait_send()


def compute_kernel(tiles, lags, land, fh, fl, ih, il, twist, eh, el, blocks, slots, mid_ref, y_ref, su_ref, sg_ref, acc_ref, lag_ref):
    def invert(s, carry):
        zz, xx, cc = s // 8, (s // 2) % 4, s % 2
        tile = tiles[s]
        slots[0, tile] = s
        slots[1, tile] = xx * 8 + zz * 2 + cc
        return carry

    lax.fori_loop(0, 32, invert, 0)
    squares = jnp.zeros((1, 128), F32)
    for kind in range(2):
        for kh in range(2):
            for arr, spec in enumerate((su_ref, sg_ref)):
                load = lambda tile, half: land[kind, kh, slots[kind, tile], arr, :, half * 128 : half * 128 + 128]
                transform(load, twist, fh, fl, mid_ref, y_ref, spec)
            multiply(su_ref, sg_ref, acc_ref, kh == 0)
        values = to_lags(acc_ref, ih, il, twist, eh, el)
        lag_ref[kind] = values
        squares = squares + jnp.sum(values * values, axis=0, keepdims=True)

    def pack(s, carry):
        zz, xx, cc = s // 8, (s // 2) % 4, s % 2
        block = lags[s]
        for kind in range(2):
            for half in range(2):
                blocks[xx, cc, zz, pl.ds(2 * kind + half, 1), :] = lag_ref[kind, pl.ds(half * 32 + block, 1), :]
        blocks[xx, cc, zz, pl.ds(4, 1), :] = squares
        return carry

    lax.fori_loop(0, 32, pack, 0)


def owners_kernel(blocks, out, total, mid, land, tally, sums, s_a, r_a, s_b, r_b, s_q, r_q, l_a, l_b):
    z, x, c = place()
    ch = lax.axis_index("ch")
    barrier = pltpu.get_barrier_semaphore()
    moves = MOVES
    far = [(dz, dy) for dz in HOPS for dy in HOPS if (dz, dy) != (0, 0)]

    def at(zz, xx, cc, yy):
        return (zz * 8 + xx * 2 + cc, yy)

    peers = [at(z, (x + d) % SIDE, (c + k) % 2, ch) for d, k in moves]
    peers += [at((z + dz) % SIDE, x, c, (ch + dy) % SIDE) for dz, dy in far]
    for peer in peers:
        pl.semaphore_signal(barrier, inc=1, device_id=peer, device_id_type=MESH)
    pl.semaphore_wait(barrier, len(peers))

    def send_a(move):
        d, k = moves[move]
        to_x, to_c = (x + d) % SIDE, (c + k) % 2
        return pltpu.make_async_remote_copy(
            src_ref=blocks.at[to_x, to_c],
            dst_ref=mid.at[:, x * 2 + c],
            send_sem=s_a.at[move],
            recv_sem=r_a.at[move],
            device_id=at(z, to_x, to_c, ch),
            device_id_type=MESH,
        )

    def send_b(hop):
        to_z = (z + HOPS[hop]) % SIDE
        return pltpu.make_async_remote_copy(
            src_ref=mid.at[to_z],
            dst_ref=land.at[z],
            send_sem=s_b.at[hop],
            recv_sem=r_b.at[hop],
            device_id=at(to_z, x, c, ch),
            device_id_type=MESH,
        )

    def send_q(k):
        dz, dy = far[k]
        return pltpu.make_async_remote_copy(
            src_ref=sums,
            dst_ref=tally.at[k],
            send_sem=s_q.at[k],
            recv_sem=r_q.at[k],
            device_id=at((z + dz) % SIDE, x, c, (ch + dy) % SIDE),
            device_id_type=MESH,
        )

    own_a = pltpu.make_async_copy(blocks.at[x, c], mid.at[:, x * 2 + c], l_a)
    own_a.start()
    for move in range(len(moves)):
        send_a(move).start()
    own_a.wait()
    for move in range(len(moves)):
        send_a(move).wait_recv()
    own_b = pltpu.make_async_copy(mid.at[z], land.at[z], l_b)
    own_b.start()
    for hop in range(3):
        send_b(hop).start()
    sums[...] = jnp.sum(mid[0], axis=0)
    for k in range(len(far)):
        send_q(k).start()
    own_b.wait()
    for hop in range(3):
        send_b(hop).wait_recv()

    for s in range(32):
        zz, xc = s // 8, s % 8
        xx, cc = xc // 2, xc % 2
        for kind in range(2):
            row = (2 * xx + cc) * 4 + zz if kind == 0 else 32 + (2 * zz + cc) * 4 + xx
            for half in range(2):
                out[row : row + 1, half * 128 : half * 128 + 128] = land[zz, xc, 2 * kind + half : 2 * kind + half + 1, :]
    for k in range(len(far)):
        send_q(k).wait_recv()
    total[...] = (sums[...] + jnp.sum(tally[...], axis=0))[4:5]
    for move in range(len(moves)):
        send_a(move).wait_send()
    for hop in range(3):
        send_b(hop).wait_send()
    for k in range(len(far)):
        send_q(k).wait_send()


def shards(inputs, out_grads, tile_order, lag_order):
    vmem = pl.BlockSpec(memory_space=pltpu.VMEM)
    smem = pl.BlockSpec(memory_space=pltpu.SMEM)
    hbm = pl.BlockSpec(memory_space=pl.ANY)
    dma = pltpu.SemaphoreType.DMA
    sds = jax.ShapeDtypeStruct
    land = pl.pallas_call(
        exchange_kernel,
        out_shape=sds((2, 2, 4, 8, 2, 8, 256), F32),
        in_specs=[hbm, hbm],
        out_specs=vmem,
        scratch_shapes=[
            pltpu.VMEM((16, 256, 128), F32),
            pltpu.VMEM((2, 4, 2, 4, 2, 2, 8, 256), F32),
            pltpu.VMEM((2, 2, 4, 8, 2, 8, 256), F32),
            dma((16,)), dma((2, 2, 7)), dma((2, 2, 7)), dma((2, 2, 3)), dma((2, 2, 3)), dma((2, 2)), dma((2, 2)),
        ],
        compiler_params=pltpu.CompilerParams(collective_id=0, has_side_effects=True),
    )(inputs, out_grads)
    (fh, fl), (ih, il), twist, (eh, el) = tables()
    consts = [jnp.asarray(t) for t in (fh, fl, ih, il, twist, eh, el)]
    blocks = pl.pallas_call(
        compute_kernel,
        out_shape=sds((4, 2, 4, 8, 128), F32),
        in_specs=[smem, smem, vmem] + [vmem] * 7,
        out_specs=vmem,
        scratch_shapes=[
            pltpu.SMEM((2, 32), jnp.int32),
            pltpu.VMEM((8, 8, 2, 8, 128), F32),
            pltpu.VMEM((ROWS, 8, 256), F32),
            pltpu.VMEM((ROWS, 8, 256), F32),
            pltpu.VMEM((ROWS, 8, 256), F32),
            pltpu.VMEM((ROWS, 8, 256), F32),
            pltpu.VMEM((2, ROWS, 128), F32),
        ],
    )(tile_order, lag_order, land.reshape(2, 2, 32, 2, 8, 256), *consts)
    owned, total = pl.pallas_call(
        owners_kernel,
        out_shape=(sds((64, 256), F32), sds((1, 128), F32)),
        in_specs=[vmem],
        out_specs=(vmem, vmem),
        scratch_shapes=[
            pltpu.VMEM((4, 8, 8, 128), F32),
            pltpu.VMEM((4, 8, 8, 128), F32),
            pltpu.VMEM((15, 8, 128), F32),
            pltpu.VMEM((8, 128), F32),
            dma((7,)), dma((7,)), dma((3,)), dma((3,)), dma((15,)), dma((15,)), dma, dma,
        ],
        compiler_params=pltpu.CompilerParams(collective_id=1, has_side_effects=True),
    )(blocks)
    squares = jnp.sum(total)
    total_entries = C // GROUP * POS // 2
    factor = target_ratio * math.sqrt(total_entries) / jnp.sqrt(squares + epsilon)
    return owned * factor


def solution(mesh):
    return jax.shard_map(
        shards,
        mesh=mesh,
        in_specs=(P("seq", "ch"), P("seq", "ch"), P(), P()),
        out_specs=P("ch", "seq"),
        check_vma=False,
    )
```

time: 863 us -> 64.6 us (0.07)
  other arithmetic: 210 us -> 2.72 us
  waiting for transfers between devices: 186 us -> 0 us
  matrix products: 169 us -> 0 us
  local copies, waits for them, and re-layouts: 110 us -> 0 us
  loops' own time: 102 us -> 0 us
  blocking collectives: 66 us -> 0 us
  Pallas kernels: 0 us -> 61 us
  between operations: 14.2 us -> 0.71 us
    dot_general x65 -> x0, matrix products: 169 us -> none  [the longest x33 106 us: spectrum(): jnp.dot(transform, values, precision=highest, preferred_element_type=jnp....]
    all_gather x1 -> x0, waiting for transfers between devices: 109 us -> none  [shards(): pieces = lax.all_gather(inputs, 'seq', axis=0, tiled=True)]
    another operation x1 -> x0, loops' own time: 102 us -> none  [shards(): lax.scan(visit_tile, zeroed, (stacked, lax.iota(jnp.int32, count_rows //...]
    dynamic_update_slice x64 -> x0, other arithmetic: 95.5 us -> none  [add_pair(): lax.dynamic_update_slice_in_dim(carried, lax.dynamic_slice_in_dim(carried...]
    reduce_scatter x1 -> x0, waiting for transfers between devices: 76.4 us -> none  [shards(): owned = lax.psum_scatter(reordered, 'seq', scatter_dimension=1, tiled=True)]
    reduce_sum x33 -> x1, other arithmetic: 71.9 us -> 1.24 us  [shards(): squares = jnp.sum(total)]
    psum x1 -> x0, blocking collectives: 66 us -> none  [shards(): squares = lax.psum(jnp.sum(owned * owned), ('seq', 'ch'))]
    pallas_call x0 -> x3, Pallas kernels: none -> 61 us  [the longest x1 34.2 us: shards(): pl.pallas_call(exchange_kernel, out_shape=sds((2, 2, 4, 8, 2, 8, 256), F3...]
  transfers between devices with their start and end apart: 2 -> 0, of which waited for: 2 -> 0; matrix products, arithmetic and copies ran while one was open for 1% -> 0% of each run, Pallas kernels for 0% -> 0%
where the time goes in v1:
time: 64.6 us; the launch traced here: 64.4 us
  Pallas kernels  61 us (94%)
  other arithmetic  2.72 us (4%)
  between operations  0.71 us (1%)
    pallas_call x1, Pallas kernels, shards(): pl.pallas_call(exchange_kernel, out_shape=sds((2, 2, 4, 8, 2, 8, 256), F3...  34.2 us
    pallas_call x1, Pallas kernels, shards(): pl.pallas_call(owners_kernel, out_shape=(sds((64, 256), F32), sds((1, 128...  14.4 us
    pallas_call x1, Pallas kernels, shards(): pl.pallas_call(compute_kernel, out_shape=sds((4, 2, 4, 8, 128), F32), in_...  12.4 us
    mul x1, other arithmetic, shards(): return owned * factor  1.48 us

profile of v1, /device:TPU:1, one launch (start us, length us, event | category | flops | bytes accessed | tf_op | source)
XLA Modules:
  0.0 64.4 jit_solution(16662887618716925665)
XLA Ops:
  0.0 34.2 %shard_map.109 = f32[2,2,4,8,2,8,256]{6,5,4,3,2,1,0:T(8,128)} custom-call(f32[256,1024]{1,0:T(8,128)} %u_ref.1, f32[256,1024]{1,0:T(8,128)} %g_ref.1), custom_call_target="tpu_custom_call" | custom-call | tf_op jit(solution)/shard_map/pallas_call | solution.py:385
  34.2 12.4 %shard_map.110.blocks = f32[4,2,4,8,128]{4,3,2,1,0:T(8,128)} custom-call(s32[32]{0:T(128)} %tiles.1, s32[32]{0:T(128)} %lags.1, f32[2,2,32,2,8,256]{5,4,3,2,1,0:T(8,128)} %bitcast.1, bf16[256,256]{1,0:T(8,128)(2,1)} %constant.20.clone.fh, bf16[256,256]{1,0:T(8,128)(2,1)} %constant.21.clone.fl, bf16[256,256]{1,0:T(8,128)(2,1)} %constant.22.clone.ih, ...), custom_call_target="tpu_custom_call" | custom-call | tf_op jit(solution)/shard_map/pallas_call | solution.py:400
  46.6 14.4 %shard_map.111 = (f32[64,256]{1,0:T(8,128)}, f32[1,128]{1,0:T(1,128)}) custom-call(f32[4,2,4,8,128]{4,3,2,1,0:T(8,128)} %shard_map.110.blocks), custom_call_target="tpu_custom_call" | custom-call | tf_op jit(solution)/shard_map/pallas_call | solution.py:415
  61.0 1.2 %reduce_sum.9 = f32[]{:T(128)} reduce(f32[1,128]{1,0:T(1,128)} %get-tuple-element.8, f32[]{:T(128)} %constant.8.clone.1), dimensions={0,1}, to_apply=%region_0.0 | reduce | flops 127 | bytes 520 | tf_op jit(solution)/shard_map/reduce_sum | solution.py:429
  62.9 1.5 %broadcast_multiply_fusion = f32[64,256]{1,0:T(8,128)} fusion(f32[64,256]{1,0:T(8,128)} %get-tuple-element.7, f32[]{:T(128)S(6)} %div.3), kind=kLoop, calls=%fused_computation | loop fusion | flops 16384 | bytes 131076 | tf_op jit(solution)/shard_map/mul | solution.py:432

commit v2 on v1

v2 whole, which is shorter than its diff:
```python
import functools
import math

import jax
import jax.numpy as jnp
import numpy as np
from jax import lax
from jax.experimental import pallas as pl
from jax.experimental.pallas import tpu as pltpu
from jax.sharding import PartitionSpec as P

C = 4096
GROUP = 16
target_ratio = 0.5
epsilon = 1e-12

MESH = pl.DeviceIdType.MESH
F32, BF16 = jnp.float32, jnp.bfloat16
SIDE = 4
POS = 16384
ROWS = 64
HOPS = (2, 1, 3, 0)
MOVES = tuple((d, k) for d in HOPS for k in (0, 1) if (d, k) != (0, 0))


def split(values):
    high = values.astype(BF16)
    return high, (values - high.astype(F32)).astype(BF16)


def dot3(left, right_high, right_low):
    high, low = split(left)
    dot = functools.partial(jnp.dot, preferred_element_type=F32)
    return dot(high, right_high) + (dot(low, right_high) + dot(high, right_low))


def tables():
    def halves(values):
        high = np.asarray(values, np.float32).astype(jnp.bfloat16)
        return high, (np.asarray(values, np.float32) - high.astype(np.float32)).astype(jnp.bfloat16)

    r = np.arange(128)
    angle = 2 * np.pi * (np.outer(r, r) % 128) / 128
    cos, sin = np.cos(angle), np.sin(angle)
    forward = np.block([[cos, -sin], [sin, cos]])
    inverse = np.block([[cos, sin], [-sin, cos]])
    m, n = np.divmod(np.arange(ROWS), 8)
    odd = 2 * (16 * n + m) + 1
    turn = np.pi * np.outer(odd, r) / POS
    twist = np.concatenate([np.cos(turn), np.sin(turn)], axis=1).astype(np.float32)
    step = 2 * np.arange(32)[None, :] + np.arange(2)[:, None]
    outer = np.pi * (np.outer(step.reshape(-1), odd) % 256) / 128
    ends = np.concatenate([np.cos(outer), -np.sin(outer)], axis=1) / (POS // 2)
    return halves(forward), halves(inverse), twist, halves(ends)


def place():
    me = lax.axis_index("seq")
    return me // 8, (me // 2) % 4, me % 2


def cmul(a, b, wr, wi):
    return a * wr - b * wi, a * wi + b * wr


def first_step(x):
    root = math.sqrt(0.5)
    s = [x[p + 4] * root for p in range(4)]
    plus = [x[p] + s[p] for p in range(4)]
    minus = [x[p] - s[p] for p in range(4)]
    out = [None] * 8
    for m in range(4):
        v = []
        for p in range(4):
            re = plus[p] if m in (0, 3) else minus[p]
            im = s[p]
            sign = -1.0 if m in (0, 1) else 1.0
            if p == 0:
                v.append((re, im if sign > 0 else -im))
            else:
                a = math.pi * (2 * m + 1) * p / 16
                wr, wi = math.cos(a), -math.sin(a)
                v.append((re * wr - im * (sign * wi), re * wi + im * (sign * wr)))
        e = (v[0][0] + v[2][0], v[0][1] + v[2][1])
        d = (v[0][0] - v[2][0], v[0][1] - v[2][1])
        f = (v[1][0] + v[3][0], v[1][1] + v[3][1])
        h = (v[1][0] - v[3][0], v[1][1] - v[3][1])
        out[m] = (e[0] + f[0], e[1] + f[1])
        out[m + 4] = (d[0] + h[1], d[1] - h[0])
    return out


def eight(z):
    add = lambda a, b: (a[0] + b[0], a[1] + b[1])
    sub = lambda a, b: (a[0] - b[0], a[1] - b[1])
    turn = lambda a: (a[1], -a[0])

    def four(a, b, c, d):
        e, f, g, h = add(a, c), sub(a, c), add(b, d), turn(sub(b, d))
        return add(e, g), add(f, h), sub(e, g), sub(f, h)

    even, odd = four(z[0], z[2], z[4], z[6]), four(z[1], z[3], z[5], z[7])
    root = math.sqrt(0.5)
    o1 = ((odd[1][0] + odd[1][1]) * root, (odd[1][1] - odd[1][0]) * root)
    o3 = ((odd[3][1] - odd[3][0]) * root, -(odd[3][0] + odd[3][1]) * root)
    turned = (odd[0], o1, turn(odd[2]), o3)
    return [add(even[k], turned[k]) for k in range(4)] + [sub(even[k], turned[k]) for k in range(4)]


def outer_steps(load, twist_ref, mid_ref, y_ref):
    def first(q2, carry):
        for half in range(2):
            out = first_step([load(4 * p + q2, half) for p in range(8)])
            for m in range(8):
                mid_ref[m, 2 * q2 + half, 0] = out[m][0]
                mid_ref[m, 2 * q2 + half, 1] = out[m][1]
        return carry

    lax.fori_loop(0, 4, first, 0)
    for m in range(8):
        z = []
        for q in range(8):
            re, im = mid_ref[m, q, 0], mid_ref[m, q, 1]
            a = math.pi * (2 * m + 1) * q / 128
            z.append((re, im) if q == 0 else cmul(re, im, math.cos(a), -math.sin(a)))
        for n, (re, im) in enumerate(eight(z)):
            row = 8 * m + n
            wr = twist_ref[pl.ds(row, 1), 0:128]
            wi = twist_ref[pl.ds(row, 1), 128:256]
            a, b = cmul(re, im, wr, -wi)
            y_ref[row, :, 0:128] = a
            y_ref[row, :, 128:256] = b


def transform(load, twist_ref, fh_ref, fl_ref, mid_ref, y_ref, spec_ref):
    outer_steps(load, twist_ref, mid_ref, y_ref)

    def rows(t, carry):
        at = pl.ds(t * 32, 32)
        spec_ref[at] = dot3(y_ref[at].reshape(256, 256), fh_ref[...], fl_ref[...]).reshape(32, 8, 256)
        return carry

    lax.fori_loop(0, ROWS // 32, rows, 0)


def multiply(u_ref, g_ref, acc_ref, fresh):
    def rows(t, carry):
        at = pl.ds(t * 4, 4)
        ur, ui = u_ref[at, :, 0:128], u_ref[at, :, 128:256]
        gr, gi = g_ref[at, :, 0:128], g_ref[at, :, 128:256]
        re, im = gr * ur + gi * ui, gi * ur - gr * ui
        if not fresh:
            re, im = re + acc_ref[at, :, 0:128], im + acc_ref[at, :, 128:256]
        acc_ref[at, :, 0:128] = re
        acc_ref[at, :, 128:256] = im
        return carry

    lax.fori_loop(0, ROWS // 4, rows, 0)


def to_lags(acc_ref, ih_ref, il_ref, twist_ref, eh_ref, el_ref):
    sums = jnp.sum(acc_ref[...], axis=1)
    v = dot3(sums, ih_ref[...], il_ref[...])
    re, im = cmul(v[:, 0:128], v[:, 128:256], twist_ref[:, 0:128], twist_ref[:, 128:256])
    high, low = split(jnp.concatenate([re, im], axis=0))
    dot = functools.partial(jnp.dot, preferred_element_type=F32)
    return dot(eh_ref[...], high) + (dot(eh_ref[...], low) + dot(el_ref[...], high))


def fused_kernel(tiles, lags, u_ref, g_ref, *refs):
    tables_hbm, refs = refs[:7], refs[7:]
    out, refs = refs[0], refs[1:]
    tables_vmem, refs = refs[:7], refs[7:]
    fh, fl, ih, il, twist, eh, el = tables_vmem
    (slots, xin, turned, mid, land, stage, mid_ref, y_ref, su_ref, sg_ref, acc_ref, lag_ref, blocks, mid_o, land_o, tally, sums,
     insem, tabsem, s_a, r_a, s_b, r_b, l_a, l_b, s_ao, r_ao, s_bo, r_bo, s_q, r_q, l_o) = refs
    z, x, c = place()
    ch = lax.axis_index("ch")

    def at(dz, dx, dc, dy):
        return (((z + dz) % SIDE) * 8 + ((x + dx) % SIDE) * 2 + (c + dc) % 2, (ch + dy) % SIDE)

    def shift(kind, d, k, e):
        return at(e, d, k, 0) if kind == 0 else at(d, e, k, 0)

    mine = ((x, z), (z, x))
    incoming = []
    for arr, ref in enumerate((u_ref, g_ref)):
        for step in HOPS:
            for kind in range(2):
                a = (mine[kind][0] + step) % SIDE
                n = len(incoming)
                copy = pltpu.make_async_copy(
                    ref.at[:, pl.ds(pl.multiple_of(kind * 512 + a * 128, 128), 128)], xin.at[n], insem.at[n]
                )
                copy.start()
                incoming.append((copy, step, kind, a, arr))
    table_copies = [pltpu.make_async_copy(h, v, tabsem.at[n]) for n, (h, v) in enumerate(zip(tables_hbm, tables_vmem))]
    for copy in table_copies:
        copy.start()

    far = [(dz, dy) for dz in HOPS for dy in HOPS if (dz, dy) != (0, 0)]
    peers = {(0, d, k, 0) for d, k in MOVES} | {(d, 0, k, 0) for d, k in MOVES} | {(dz, 0, 0, dy) for dz, dy in far}
    peers = sorted(peers)
    barrier = pltpu.get_barrier_semaphore()
    for peer in peers:
        pl.semaphore_signal(barrier, inc=1, device_id=at(*peer), device_id_type=MESH)
    pl.semaphore_wait(barrier, len(peers))

    def send_a(kind, kh, arr, move):
        d, k = MOVES[move]
        a = mine[kind][0]
        return pltpu.make_async_remote_copy(
            src_ref=turned.at[kind, (a + d) % SIDE, (c + k) % 2, :, kh, arr],
            dst_ref=mid.at[kind, kh, arr, :, a * 2 + c],
            send_sem=s_a.at[kind, kh, arr, move],
            recv_sem=r_a.at[kind, kh, arr, move],
            device_id=shift(kind, d, k, 0),
            device_id_type=MESH,
        )

    def own_a(kind, kh, arr):
        a = mine[kind][0]
        return pltpu.make_async_copy(
            turned.at[kind, a, c, :, kh, arr], mid.at[kind, kh, arr, :, a * 2 + c], l_a.at[kind, kh, arr]
        )

    def send_b(kind, kh, arr, hop):
        b = mine[kind][1]
        return pltpu.make_async_remote_copy(
            src_ref=mid.at[kind, kh, arr, (b + HOPS[hop]) % SIDE],
            dst_ref=land.at[kind, kh, arr, pl.ds(b * 8, 8)],
            send_sem=s_b.at[kind, kh, arr, hop],
            recv_sem=r_b.at[kind, kh, arr, hop],
            device_id=shift(kind, 0, 0, HOPS[hop]),
            device_id_type=MESH,
        )

    def own_b(kind, kh, arr):
        b = mine[kind][1]
        return pltpu.make_async_copy(
            mid.at[kind, kh, arr, b], land.at[kind, kh, arr, pl.ds(b * 8, 8)], l_b.at[kind, kh, arr]
        )

    for n, (copy, step, kind, a, arr) in enumerate(incoming):
        copy.wait()
        turned[kind, a, :, :, :, arr] = xin[n].T.reshape(2, 4, 2, 8, 256)
        for move, (d, k) in enumerate(MOVES):
            if d == step:
                send_a(kind, 0, arr, move).start()
        if step == 0:
            own_a(kind, 0, arr).start()
    for arr in range(2):
        for move in range(len(MOVES)):
            for kind in range(2):
                send_a(kind, 1, arr, move).start()
        for kind in range(2):
            own_a(kind, 1, arr).start()

    def find(tile, carry):
        first, second = jnp.int32(0), jnp.int32(0)
        for s in range(32):
            zz, xx, cc = s // 8, (s // 2) % 4, s % 2
            hit = tiles[s] == tile
            first = jnp.where(hit, s, first)
            second = jnp.where(hit, xx * 8 + zz * 2 + cc, second)
        slots[0, tile] = first
        slots[1, tile] = second
        return carry

    lax.fori_loop(0, 32, find, 0)

    for kh in range(2):
        for arr in range(2):
            for kind in range(2):
                own_a(kind, kh, arr).wait()
                for move in range(len(MOVES)):
                    send_a(kind, kh, arr, move).wait_recv()
                for hop in range(3):
                    send_b(kind, kh, arr, hop).start()
                own_b(kind, kh, arr).start()
    for copy in table_copies:
        copy.wait()
    acc_ref[...] = jnp.zeros_like(acc_ref)

    def chunk(kh, carry):
        for arr, spec in enumerate((su_ref, sg_ref)):
            for kind in range(2):
                own_b(kind, kh, arr).wait()
                for hop in range(3):
                    send_b(kind, kh, arr, hop).wait_recv()
                stage[...] = land[kind, kh, arr]
                load = lambda tile, half: stage[slots[kind, tile], :, half * 128 : half * 128 + 128]
                transform(load, twist, fh, fl, mid_ref, y_ref, spec.at[kind])
                if arr == 1:
                    multiply(su_ref.at[kind], sg_ref.at[kind], acc_ref.at[kind], False)
        return carry

    lax.fori_loop(0, 2, chunk, 0)
    squares = jnp.zeros((1, 128), F32)
    for kind in range(2):
        values = to_lags(acc_ref.at[kind], ih, il, twist, eh, el)
        lag_ref[kind] = values
        squares = squares + jnp.sum(values * values, axis=0, keepdims=True)

    def send_ao(move):
        d, k = MOVES[move]
        return pltpu.make_async_remote_copy(
            src_ref=blocks.at[(x + d) % SIDE, (c + k) % 2],
            dst_ref=mid_o.at[:, x * 2 + c],
            send_sem=s_ao.at[move],
            recv_sem=r_ao.at[move],
            device_id=at(0, d, k, 0),
            device_id_type=MESH,
        )

    def send_bo(hop):
        return pltpu.make_async_remote_copy(
            src_ref=mid_o.at[(z + HOPS[hop]) % SIDE],
            dst_ref=land_o.at[z],
            send_sem=s_bo.at[hop],
            recv_sem=r_bo.at[hop],
            device_id=at(HOPS[hop], 0, 0, 0),
            device_id_type=MESH,
        )

    def send_q(k):
        return pltpu.make_async_remote_copy(
            src_ref=sums,
            dst_ref=tally.at[k],
            send_sem=s_q.at[k],
            recv_sem=r_q.at[k],
            device_id=at(far[k][0], 0, 0, far[k][1]),
            device_id_type=MESH,
        )

    def pack(s, carry):
        zz, xx, cc = s // 8, (s // 2) % 4, s % 2
        block = lags[s]
        for kind in range(2):
            for half in range(2):
                blocks[xx, cc, zz, pl.ds(2 * kind + half, 1), :] = lag_ref[kind, pl.ds(half * 32 + block, 1), :]
        blocks[xx, cc, zz, pl.ds(4, 1), :] = squares
        return carry

    lax.fori_loop(0, 32, pack, 0)
    own_ao = pltpu.make_async_copy(blocks.at[x, c], mid_o.at[:, x * 2 + c], l_o.at[0])
    own_ao.start()
    for move in range(len(MOVES)):
        send_ao(move).start()
    own_ao.wait()
    for move in range(len(MOVES)):
        send_ao(move).wait_recv()
    own_bo = pltpu.make_async_copy(mid_o.at[z], land_o.at[z], l_o.at[1])
    own_bo.start()
    for hop in range(3):
        send_bo(hop).start()
    sums[...] = jnp.sum(mid_o[0], axis=0)
    for k in range(len(far)):
        send_q(k).start()
    for kh in range(2):
        for arr in range(2):
            for kind in range(2):
                for move in range(len(MOVES)):
                    send_a(kind, kh, arr, move).wait_send()
                for hop in range(3):
                    send_b(kind, kh, arr, hop).wait_send()
    for move in range(len(MOVES)):
        send_ao(move).wait_send()
    for k in range(len(far)):
        send_q(k).wait_recv()
    total = jnp.sum((sums[...] + jnp.sum(tally[...], axis=0))[4:5], axis=1, keepdims=True)
    total_entries = C // GROUP * POS // 2
    factor = target_ratio * math.sqrt(total_entries) / jnp.sqrt(total + epsilon)
    own_bo.wait()
    for hop in range(3):
        send_bo(hop).wait_recv()
    for s in range(32):
        zz, xc = s // 8, s % 8
        xx, cc = xc // 2, xc % 2
        for kind in range(2):
            row = (2 * xx + cc) * 4 + zz if kind == 0 else 32 + (2 * zz + cc) * 4 + xx
            for half in range(2):
                values = land_o[zz, xc, 2 * kind + half : 2 * kind + half + 1, :]
                out[row : row + 1, half * 128 : half * 128 + 128] = values * factor
    for hop in range(3):
        send_bo(hop).wait_send()
    for k in range(len(far)):
        send_q(k).wait_send()


def shards(inputs, out_grads, tile_order, lag_order):
    vmem = pl.BlockSpec(memory_space=pltpu.VMEM)
    smem = pl.BlockSpec(memory_space=pltpu.SMEM)
    hbm = pl.BlockSpec(memory_space=pl.ANY)
    dma = pltpu.SemaphoreType.DMA
    (fh, fl), (ih, il), twist, (eh, el) = tables()
    consts = [jnp.asarray(t) for t in (fh, fl, ih, il, twist, eh, el)]
    return pl.pallas_call(
        fused_kernel,
        out_shape=jax.ShapeDtypeStruct((64, 256), F32),
        in_specs=[smem, smem] + [hbm] * 9,
        out_specs=vmem,
        scratch_shapes=[pltpu.VMEM(t.shape, t.dtype) for t in consts]
        + [
            pltpu.SMEM((2, 32), jnp.int32),
            pltpu.VMEM((16, 256, 128), F32),
            pltpu.VMEM((2, 4, 2, 4, 2, 2, 8, 256), F32),
            pltpu.VMEM((2, 2, 2, 4, 8, 8, 256), F32),
            pltpu.VMEM((2, 2, 2, 32, 8, 256), F32),
            pltpu.VMEM((32, 8, 256), F32),
            pltpu.VMEM((8, 8, 2, 8, 128), F32),
            pltpu.VMEM((ROWS, 8, 256), F32),
            pltpu.VMEM((2, ROWS, 8, 256), F32),
            pltpu.VMEM((2, ROWS, 8, 256), F32),
            pltpu.VMEM((2, ROWS, 8, 256), F32),
            pltpu.VMEM((2, ROWS, 128), F32),
            pltpu.VMEM((4, 2, 4, 8, 128), F32),
            pltpu.VMEM((4, 8, 8, 128), F32),
            pltpu.VMEM((4, 8, 8, 128), F32),
            pltpu.VMEM((15, 8, 128), F32),
            pltpu.VMEM((8, 128), F32),
            dma((16,)), dma((7,)), dma((2, 2, 2, 7)), dma((2, 2, 2, 7)), dma((2, 2, 2, 3)), dma((2, 2, 2, 3)),
            dma((2, 2, 2)), dma((2, 2, 2)), dma((7,)), dma((7,)), dma((3,)), dma((3,)), dma((15,)), dma((15,)), dma((2,)),
        ],
        compiler_params=pltpu.CompilerParams(collective_id=0, has_side_effects=True),
    )(tile_order, lag_order, inputs, out_grads, *consts)


def solution(mesh):
    return jax.shard_map(
        shards,
        mesh=mesh,
        in_specs=(P("seq", "ch"), P("seq", "ch"), P(), P()),
        out_specs=P("ch", "seq"),
        check_vma=False,
    )
```

time: 64.6 us -> 51 us (0.79)
  Pallas kernels: 61 us -> 49.3 us
  other arithmetic: 2.72 us -> 0 us
  local copies, waits for them, and re-layouts: 0 us -> 1.47 us
  between operations: 0.71 us -> 0.01 us
    pallas_call x3 -> x1, Pallas kernels: 61 us -> 49.3 us  [shards(): pl.pallas_call(fused_kernel, out_shape=jax.ShapeDtypeStruct((64, 256), F3...]
    mul x1 -> x0, other arithmetic: 1.48 us -> none  [shards(): return owned * factor]
    unnamed x0 -> x1, local copies, waits for them, and re-layouts: none -> 1.47 us
    reduce_sum x1 -> x0, other arithmetic: 1.24 us -> none  [shards(): squares = jnp.sum(total)]
where the time goes in v2:
time: 51 us; the launch traced here: 50.8 us
  Pallas kernels  49.3 us (97%)
  local copies, waits for them, and re-layouts  1.47 us (3%)
    pallas_call x1, Pallas kernels, shards(): pl.pallas_call(fused_kernel, out_shape=jax.ShapeDtypeStruct((64, 256), F3...  49.3 us
    unnamed x1, local copies, waits for them, and re-layouts  1.47 us

profile of v2, /device:TPU:1, one launch (start us, length us, event | category | flops | bytes accessed | tf_op | source)
XLA Modules:
  0.0 50.8 jit_solution(17355009916190374642)
XLA Ops:
  0.0 49.3 %shard_map.109 = f32[64,256]{1,0:T(8,128)} custom-call(s32[32]{0:T(128)} %tiles.1, s32[32]{0:T(128)} %lags.1, f32[256,1024]{1,0:T(8,128)} %u_ref.1, f32[256,1024]{1,0:T(8,128)} %g_ref.1, bf16[256,256]{1,0:T(8,128)(2,1)} %constant.14.clone.refs_0_, bf16[256,256]{1,0:T(8,128)(2,1)} %constant.15.clone.refs_1_, bf16[256,256]{1,0:T(8,128)(2,1)} %constant.16.clone.refs_2_, ...), custom_call_target="tpu_custom_call" | custom-call | tf_op jit(solution)/shard_map/pallas_call | solution.py:399
  49.3 1.5 %copy.13 = f32[64,256]{1,0:T(8,128)} copy(f32[64,256]{1,0:T(8,128)} %shard_map.109) | data formatting | bytes 131072

commit v3 on v2

v3 whole, which is shorter than its diff:
```python
import functools
import math

import jax
import jax.numpy as jnp
import numpy as np
from jax import lax
from jax.experimental import pallas as pl
from jax.experimental.pallas import tpu as pltpu
from jax.sharding import PartitionSpec as P

C = 4096
GROUP = 16
target_ratio = 0.5
epsilon = 1e-12

MESH = pl.DeviceIdType.MESH
F32, BF16 = jnp.float32, jnp.bfloat16
SIDE = 4
POS = 16384
ROWS = 64
HOPS = (2, 1, 3, 0)
MOVES = tuple((d, k) for d in HOPS for k in (0, 1) if (d, k) != (0, 0))


def split(values):
    high = values.astype(BF16)
    return high, (values - high.astype(F32)).astype(BF16)


def dot3(left, right):
    dot = functools.partial(jnp.dot, preferred_element_type=F32)
    return dot(left[0], right[0]) + (dot(left[1], right[0]) + dot(left[0], right[1]))


def tables():
    def halves(values):
        high = np.asarray(values, np.float32).astype(jnp.bfloat16)
        return high, (np.asarray(values, np.float32) - high.astype(np.float32)).astype(jnp.bfloat16)

    r = np.arange(128)
    angle = 2 * np.pi * (np.outer(r, r) % 128) / 128
    cos, sin = np.cos(angle), np.sin(angle)
    forward = np.block([[cos, -sin], [sin, cos]])
    inverse = np.block([[cos, sin], [-sin, cos]])
    m, n = np.divmod(np.arange(ROWS), 8)
    odd = 2 * (16 * n + m) + 1
    turn = np.pi * np.outer(odd, r) / POS
    twist = np.concatenate([np.cos(turn), np.sin(turn)], axis=1).astype(np.float32)
    step = 2 * np.arange(32)[None, :] + np.arange(2)[:, None]
    outer = np.pi * (np.outer(step.reshape(-1), odd) % 256) / 128
    ends = np.concatenate([np.cos(outer), -np.sin(outer)], axis=1) / (POS // 2)
    return (*halves(forward), *halves(inverse), twist, ends.astype(np.float32))


def place():
    me = lax.axis_index("seq")
    return me // 8, (me // 2) % 4, me % 2


def cmul(a, b, wr, wi):
    return a * wr - b * wi, a * wi + b * wr


def first_step(x):
    root = math.sqrt(0.5)
    s = [x[p + 4] * root for p in range(4)]
    plus = [x[p] + s[p] for p in range(4)]
    minus = [x[p] - s[p] for p in range(4)]
    out = [None] * 8
    for m in range(4):
        v = []
        for p in range(4):
            re = plus[p] if m in (0, 3) else minus[p]
            im = s[p]
            sign = -1.0 if m in (0, 1) else 1.0
            if p == 0:
                v.append((re, im if sign > 0 else -im))
            else:
                a = math.pi * (2 * m + 1) * p / 16
                wr, wi = math.cos(a), -math.sin(a)
                v.append((re * wr - im * (sign * wi), re * wi + im * (sign * wr)))
        e = (v[0][0] + v[2][0], v[0][1] + v[2][1])
        d = (v[0][0] - v[2][0], v[0][1] - v[2][1])
        f = (v[1][0] + v[3][0], v[1][1] + v[3][1])
        h = (v[1][0] - v[3][0], v[1][1] - v[3][1])
        out[m] = (e[0] + f[0], e[1] + f[1])
        out[m + 4] = (d[0] + h[1], d[1] - h[0])
    return out


def eight(z):
    add = lambda a, b: (a[0] + b[0], a[1] + b[1])
    sub = lambda a, b: (a[0] - b[0], a[1] - b[1])
    turn = lambda a: (a[1], -a[0])

    def four(a, b, c, d):
        e, f, g, h = add(a, c), sub(a, c), add(b, d), turn(sub(b, d))
        return add(e, g), add(f, h), sub(e, g), sub(f, h)

    even, odd = four(z[0], z[2], z[4], z[6]), four(z[1], z[3], z[5], z[7])
    root = math.sqrt(0.5)
    o1 = ((odd[1][0] + odd[1][1]) * root, (odd[1][1] - odd[1][0]) * root)
    o3 = ((odd[3][1] - odd[3][0]) * root, -(odd[3][0] + odd[3][1]) * root)
    turned = (odd[0], o1, turn(odd[2]), o3)
    return [add(even[k], turned[k]) for k in range(4)] + [sub(even[k], turned[k]) for k in range(4)]


def outer_first(load, mid_ref):
    for q2 in range(4):
        for half in range(2):
            out = first_step([load(4 * p + q2, half) for p in range(8)])
            for m in range(8):
                mid_ref[m, 2 * q2 + half, 0] = out[m][0]
                mid_ref[m, 2 * q2 + half, 1] = out[m][1]


def outer_second(twist_ref, mid_ref, y_ref):
    for m in range(8):
        z = []
        for q in range(8):
            re, im = mid_ref[m, q, 0], mid_ref[m, q, 1]
            a = math.pi * (2 * m + 1) * q / 128
            z.append((re, im) if q == 0 else cmul(re, im, math.cos(a), -math.sin(a)))
        done = []
        for n, (re, im) in enumerate(eight(z)):
            row = 8 * m + n
            done.append(cmul(re, im, twist_ref[row : row + 1, 0:128], -twist_ref[row : row + 1, 128:256]))
        for n in range(0, 8, 2):
            for part in range(2):
                pair = split(jnp.concatenate([done[n][part], done[n + 1][part]], axis=0))
                for k in range(2):
                    y_ref[k, (8 * m + n) * 8 : (8 * m + n) * 8 + 16, part * 128 : part * 128 + 128] = pair[k]


def inner(y_ref, at, table):
    return dot3((y_ref[0, at : at + 256], y_ref[1, at : at + 256]), table)


def channel_sums(rows):
    lane = lax.broadcasted_iota(jnp.int32, (8, 128), 0)
    low = lane < 4
    out = []
    for k in range(4):
        a, b = rows[k], rows[k + 4]
        out.append(jnp.where(low, a, b) + pltpu.roll(jnp.where(low, b, a), 4, 0))
    for width in (2, 1):
        keep = lane % (2 * width) < width
        out = [
            jnp.where(keep, a + pltpu.roll(a, 8 - width, 0), b + pltpu.roll(b, width, 0))
            for a, b in zip(out[:width], out[width:])
        ]
    return out[0]


def multiply(grads, spec_ref, at, acc_ref):
    for m in range(4):
        re, im = [], []
        for n in range(8):
            row = m * 64 + n * 8
            gr, gi = grads[row : row + 8, 0:128], grads[row : row + 8, 128:256]
            ur, ui = spec_ref[at + row : at + row + 8, 0:128], spec_ref[at + row : at + row + 8, 128:256]
            re.append(gr * ur + gi * ui)
            im.append(gi * ur - gr * ui)
        to = at // 8 + m * 8
        acc_ref[to : to + 8, 0:128] += channel_sums(re)
        acc_ref[to : to + 8, 128:256] += channel_sums(im)


def fused_kernel(tiles, lags, u_ref, g_ref, *refs):
    tables_hbm, refs = refs[:6], refs[6:]
    out, refs = refs[0], refs[1:]
    tables_vmem, refs = refs[:6], refs[6:]
    fh, fl, ih, il, twist, ends = tables_vmem
    (slots, xin, turned, mid, land, stage, mid_ref, y_a, y_b, spec_ref, acc_ref, ends_f, ends_b, blocks, mid_o, land_o,
     owned, square, near_sq, sums, tally,
     insem, tabsem, s_a, r_a, s_b, r_b, l_a, l_b, s_ao, r_ao, s_bo, r_bo, s_n, r_n, s_q, r_q, l_o, far_sem) = refs
    z, x, c = place()
    ch = lax.axis_index("ch")

    def at(dz, dx, dc, dy):
        return (((z + dz) % SIDE) * 8 + ((x + dx) % SIDE) * 2 + (c + dc) % 2, (ch + dy) % SIDE)

    def shift(kind, d, k, e):
        return at(e, d, k, 0) if kind == 0 else at(d, e, k, 0)

    far = [(dz, dy) for dz in HOPS for dy in HOPS if (dz, dy) != (0, 0)]
    column = [(0, 0, 0, d) for d in HOPS[:3]]
    peers = {(0, d, k, 0) for d, k in MOVES} | {(d, 0, k, 0) for d, k in MOVES} | set(column)
    barrier = pltpu.get_barrier_semaphore()
    for peer in sorted(peers):
        pl.semaphore_signal(barrier, inc=1, device_id=at(*peer), device_id_type=MESH)

    mine = ((x, z), (z, x))
    incoming = []
    for arr, ref in enumerate((u_ref, g_ref)):
        for step in HOPS:
            for kind in range(2):
                a = (mine[kind][0] + step) % SIDE
                n = len(incoming)
                copy = pltpu.make_async_copy(
                    ref.at[:, pl.ds(pl.multiple_of(kind * 512 + a * 128, 128), 128)], xin.at[n], insem.at[n]
                )
                copy.start()
                incoming.append((copy, step, kind, a, arr))
    table_copies = [pltpu.make_async_copy(h, v, tabsem.at[n]) for n, (h, v) in enumerate(zip(tables_hbm, tables_vmem))]
    for copy in table_copies:
        copy.start()

    def send_a(kind, kh, arr, move):
        d, k = MOVES[move]
        a = mine[kind][0]
        return pltpu.make_async_remote_copy(
            src_ref=turned.at[kind, (a + d) % SIDE, (c + k) % 2, :, kh, arr],
            dst_ref=mid.at[kind, kh, arr, :, a * 2 + c],
            send_sem=s_a.at[kind, kh, arr, move],
            recv_sem=r_a.at[kind, kh, arr, move],
            device_id=shift(kind, d, k, 0),
            device_id_type=MESH,
        )

    def own_a(kind, kh, arr):
        a = mine[kind][0]
        return pltpu.make_async_copy(
            turned.at[kind, a, c, :, kh, arr], mid.at[kind, kh, arr, :, a * 2 + c], l_a.at[kind, kh, arr]
        )

    def send_b(kind, kh, arr, hop):
        b = mine[kind][1]
        return pltpu.make_async_remote_copy(
            src_ref=mid.at[kind, kh, arr, (b + HOPS[hop]) % SIDE],
            dst_ref=land.at[kind, kh, arr, pl.ds(b * 8, 8)],
            send_sem=s_b.at[kind, kh, arr, hop],
            recv_sem=r_b.at[kind, kh, arr, hop],
            device_id=shift(kind, 0, 0, HOPS[hop]),
            device_id_type=MESH,
        )

    def own_b(kind, kh, arr):
        b = mine[kind][1]
        return pltpu.make_async_copy(
            mid.at[kind, kh, arr, b], land.at[kind, kh, arr, pl.ds(b * 8, 8)], l_b.at[kind, kh, arr]
        )

    def turn(n):
        copy, step, kind, a, arr = incoming[n]
        copy.wait()
        turned[kind, a, :, :, :, arr] = xin[n].T.reshape(2, 4, 2, 8, 256)

    def begin(n):
        _, step, kind, a, arr = incoming[n]
        for move, (d, k) in enumerate(MOVES):
            if d == step:
                send_a(kind, 0, arr, move).start()

    early = 4
    for n in range(early):
        turn(n)
    pl.semaphore_wait(barrier, len(peers))
    for n in range(early):
        begin(n)
    for n in range(early, len(incoming)):
        turn(n)
        begin(n)
    for arr in range(2):
        for move in range(len(MOVES)):
            for kind in range(2):
                send_a(kind, 1, arr, move).start()
    for kh in range(2):
        for arr in range(2):
            for kind in range(2):
                own_a(kind, kh, arr).start()
    for peer in column:
        pl.semaphore_signal(far_sem, inc=1, device_id=at(*peer), device_id_type=MESH)

    def find(tile, carry):
        first, second = jnp.int32(0), jnp.int32(0)
        for s in range(32):
            zz, xx, cc = s // 8, (s // 2) % 4, s % 2
            hit = tiles[s] == tile
            first = jnp.where(hit, s, first)
            second = jnp.where(hit, xx * 8 + zz * 2 + cc, second)
        slots[0, tile] = first
        slots[1, tile] = second
        return carry

    lax.fori_loop(0, 32, find, 0)

    def forward(kh, arr):
        for kind in range(2):
            own_a(kind, kh, arr).wait()
            for move in range(len(MOVES)):
                send_a(kind, kh, arr, move).wait_recv()
            for hop in range(3):
                send_b(kind, kh, arr, hop).start()
            own_b(kind, kh, arr).start()

    forward(0, 0)
    for copy in table_copies:
        copy.wait()
    acc_ref[...] = jnp.zeros_like(acc_ref)
    for t in range(32):
        xc, zz = t // 4, t % 4
        block = lags[zz * 8 + xc]
        for half in range(2):
            ends_f[half * 32 + t : half * 32 + t + 1, :] = ends[pl.ds(half * 32 + block, 1), :]
    high, low = split(ends_f[...])
    ends_b[0] = high
    ends_b[1] = low
    forward(0, 1)
    forward(1, 0)
    forward(1, 1)
    inner_table = (fh[...], fl[...])

    def take(kind, kh, arr):
        own_b(kind, kh, arr).wait()
        for hop in range(3):
            send_b(kind, kh, arr, hop).wait_recv()
        stage[...] = land[kind, kh, arr]
        return lambda tile, half: stage[slots[kind, tile], :, half * 128 : half * 128 + 128]

    def spectra(kind, y_ref, part):
        spec_ref[kind, part * 256 : part * 256 + 256] = inner(y_ref, part * 256, inner_table)

    def products(kind, y_ref, part):
        multiply(inner(y_ref, part * 256, inner_table), spec_ref.at[kind], part * 256, acc_ref.at[kind])

    def chunk(kh, carry):
        outer_first(take(0, kh, 0), mid_ref)
        outer_second(twist, mid_ref, y_a)
        load = take(1, kh, 0)
        spectra(0, y_a, 0)
        outer_first(load, mid_ref)
        spectra(0, y_a, 1)
        outer_second(twist, mid_ref, y_b)
        load = take(0, kh, 1)
        spectra(1, y_b, 0)
        outer_first(load, mid_ref)
        spectra(1, y_b, 1)
        outer_second(twist, mid_ref, y_a)
        load = take(1, kh, 1)
        products(0, y_a, 0)
        outer_first(load, mid_ref)
        products(0, y_a, 1)
        outer_second(twist, mid_ref, y_b)
        products(1, y_b, 0)
        products(1, y_b, 1)
        return carry

    lax.fori_loop(0, 2, chunk, 0)

    back = (ih[...], il[...])
    sides = []
    for kind in range(2):
        v = dot3(split(acc_ref[kind]), back)
        re, im = cmul(v[:, 0:128], v[:, 128:256], twist[:, 0:128], twist[:, 128:256])
        sides.append(jnp.concatenate([re, im], axis=0))
    high, low = split(jnp.concatenate(sides, axis=1))
    dot = functools.partial(jnp.dot, preferred_element_type=F32)
    values = dot(ends_b[0], high) + (dot(ends_b[0], low) + dot(ends_b[1], high))

    def send_n(move):
        d, k = MOVES[move]
        return pltpu.make_async_remote_copy(
            src_ref=square,
            dst_ref=near_sq.at[x * 2 + c],
            send_sem=s_n.at[move],
            recv_sem=r_n.at[move],
            device_id=at(0, d, k, 0),
            device_id_type=MESH,
        )

    def send_q(k):
        return pltpu.make_async_remote_copy(
            src_ref=sums,
            dst_ref=tally.at[k],
            send_sem=s_q.at[k],
            recv_sem=r_q.at[k],
            device_id=at(far[k][0], 0, 0, far[k][1]),
            device_id_type=MESH,
        )

    def send_ao(move):
        d, k = MOVES[move]
        return pltpu.make_async_remote_copy(
            src_ref=blocks.at[pl.ds((((x + d) % SIDE) * 2 + (c + k) % 2) * 32, 32)],
            dst_ref=mid_o.at[x * 2 + c],
            send_sem=s_ao.at[move],
            recv_sem=r_ao.at[move],
            device_id=at(0, d, k, 0),
            device_id_type=MESH,
        )

    def send_bo(hop):
        return pltpu.make_async_remote_copy(
            src_ref=mid_o.at[:, pl.ds(((z + HOPS[hop]) % SIDE) * 8, 8)],
            dst_ref=land_o.at[pl.ds(z * 8, 8)],
            send_sem=s_bo.at[hop],
            recv_sem=r_bo.at[hop],
            device_id=at(HOPS[hop], 0, 0, 0),
            device_id_type=MESH,
        )

    both = values[:, 0:128] * values[:, 0:128] + values[:, 128:256] * values[:, 128:256]
    own_square = jnp.sum(both, axis=0, keepdims=True)
    square[...] = own_square
    for move in range(len(MOVES)):
        send_n(move).start()
    for kind in range(2):
        for half in range(2):
            blocks[pl.ds(2 * kind + half, 32, stride=8), :] = values[half * 32 : half * 32 + 32, kind * 128 : kind * 128 + 128]
    for move in range(len(MOVES)):
        send_ao(move).start()
    own_ao = pltpu.make_async_copy(blocks.at[pl.ds((x * 2 + c) * 32, 32)], mid_o.at[x * 2 + c], l_o.at[0])
    own_ao.start()
    near_sq[x * 2 + c] = own_square
    pl.semaphore_wait(far_sem, len(column))
    own_ao.wait()
    for move in range(len(MOVES)):
        send_n(move).wait_recv()
    line_sum = jnp.sum(near_sq[...], axis=0)
    sums[...] = line_sum
    for k in range(len(far)):
        send_q(k).start()
    for move in range(len(MOVES)):
        send_ao(move).wait_recv()
    for hop in range(3):
        send_bo(hop).start()
    own_bo = pltpu.make_async_copy(mid_o.at[:, pl.ds(z * 8, 8)], land_o.at[pl.ds(z * 8, 8)], l_o.at[1])
    own_bo.start()
    for kh in range(2):
        for arr in range(2):
            for kind in range(2):
                for move in range(len(MOVES)):
                    send_a(kind, kh, arr, move).wait_send()
                for hop in range(3):
                    send_b(kind, kh, arr, hop).wait_send()
    for move in range(len(MOVES)):
        send_ao(move).wait_send()
        send_n(move).wait_send()
    own_bo.wait()
    for hop in range(3):
        send_bo(hop).wait_recv()
    rows = land_o.reshape(256, 128)
    for zz in range(4):
        for half in range(2):
            owned[pl.ds(half * 64 + zz, 8, stride=4), :] = rows[pl.ds(zz * 64 + half, 8, stride=8), :]
            for cc in range(2):
                to = half * 64 + 32 + 8 * zz + 4 * cc
                owned[to : to + 4, :] = rows[pl.ds(zz * 64 + cc * 8 + 2 + half, 4, stride=16), :]
    for hop in range(3):
        send_bo(hop).wait_send()
    for k in range(len(far)):
        send_q(k).wait_send()
    for k in range(len(far)):
        send_q(k).wait_recv()
    total = jnp.sum(line_sum + jnp.sum(tally[...], axis=0), axis=1, keepdims=True)
    total_entries = C // GROUP * POS // 2
    factor = target_ratio * math.sqrt(total_entries) / jnp.sqrt(total + epsilon)
    out[:, 0:128] = owned[0:64] * factor
    out[:, 128:256] = owned[64:128] * factor


def shards(inputs, out_grads, tile_order, lag_order):
    vmem = pl.BlockSpec(memory_space=pltpu.VMEM)
    smem = pl.BlockSpec(memory_space=pltpu.SMEM)
    hbm = pl.BlockSpec(memory_space=pl.ANY)
    dma = pltpu.SemaphoreType.DMA
    consts = [jnp.asarray(t) for t in tables()]
    return pl.pallas_call(
        fused_kernel,
        out_shape=jax.ShapeDtypeStruct((64, 256), F32),
        in_specs=[smem, smem] + [hbm] * 8,
        out_specs=vmem,
        scratch_shapes=[pltpu.VMEM(t.shape, t.dtype) for t in consts]
        + [
            pltpu.SMEM((2, 32), jnp.int32),
            pltpu.VMEM((16, 256, 128), F32),
            pltpu.VMEM((2, 4, 2, 4, 2, 2, 8, 256), F32),
            pltpu.VMEM((2, 2, 2, 4, 8, 8, 256), F32),
            pltpu.VMEM((2, 2, 2, 32, 8, 256), F32),
            pltpu.VMEM((32, 8, 256), F32),
            pltpu.VMEM((8, 8, 2, 8, 128), F32),
            pltpu.VMEM((2, ROWS * 8, 256), BF16),
            pltpu.VMEM((2, ROWS * 8, 256), BF16),
            pltpu.VMEM((2, ROWS * 8, 256), F32),
            pltpu.VMEM((2, ROWS, 256), F32),
            pltpu.VMEM((ROWS, 128), F32),
            pltpu.VMEM((2, ROWS, 128), BF16),
            pltpu.VMEM((256, 128), F32),
            pltpu.VMEM((8, 32, 128), F32),
            pltpu.VMEM((32, 8, 128), F32),
            pltpu.VMEM((128, 128), F32),
            pltpu.VMEM((1, 128), F32),
            pltpu.VMEM((8, 1, 128), F32),
            pltpu.VMEM((1, 128), F32),
            pltpu.VMEM((15, 1, 128), F32),
            dma((16,)), dma((6,)), dma((2, 2, 2, 7)), dma((2, 2, 2, 7)), dma((2, 2, 2, 3)), dma((2, 2, 2, 3)),
            dma((2, 2, 2)), dma((2, 2, 2)), dma((7,)), dma((7,)), dma((3,)), dma((3,)), dma((7,)), dma((7,)),
            dma((15,)), dma((15,)), dma((2,)), pltpu.SemaphoreType.REGULAR,
        ],
        compiler_params=pltpu.CompilerParams(collective_id=0, has_side_effects=True),
    )(tile_order, lag_order, inputs, out_grads, *consts)


def solution(mesh):
    return jax.shard_map(
        shards,
        mesh=mesh,
        in_specs=(P("seq", "ch"), P("seq", "ch"), P(), P()),
        out_specs=P("ch", "seq"),
        check_vma=False,
    )
```

time: 51 us -> 47.4 us (0.929)
  Pallas kernels: 49.3 us -> 45.6 us
    pallas_call x1, Pallas kernels: 49.3 us -> 45.6 us  [shards(): pl.pallas_call(fused_kernel, out_shape=jax.ShapeDtypeStruct((64, 256), F3...]
where the time goes in v3:
time: 47.4 us; the launch traced here: 47.1 us
  Pallas kernels  45.6 us (96%)
  local copies, waits for them, and re-layouts  1.47 us (3%)
    pallas_call x1, Pallas kernels, shards(): pl.pallas_call(fused_kernel, out_shape=jax.ShapeDtypeStruct((64, 256), F3...  45.6 us
    unnamed x1, local copies, waits for them, and re-layouts  1.47 us

profile of v3, /device:TPU:1, one launch (start us, length us, event | category | flops | bytes accessed | tf_op | source)
XLA Modules:
  0.0 47.1 jit_solution(6634519763504532507)
XLA Ops:
  0.0 45.6 %shard_map.100 = f32[64,256]{1,0:T(8,128)} custom-call(s32[32]{0:T(128)} %tiles.1, s32[32]{0:T(128)} %lags.1, f32[256,1024]{1,0:T(8,128)} %u_ref.1, f32[256,1024]{1,0:T(8,128)} %g_ref.1, bf16[256,256]{1,0:T(8,128)(2,1)} %constant.12.clone.refs_0_, bf16[256,256]{1,0:T(8,128)(2,1)} %constant.13.clone.refs_1_, bf16[256,256]{1,0:T(8,128)(2,1)} %constant.14.clone.refs_2_, ...), custom_call_target="tpu_custom_call" | custom-call | tf_op jit(solution)/shard_map/pallas_call | solution.py:470
  45.6 1.5 %copy.12 = f32[64,256]{1,0:T(8,128)} copy(f32[64,256]{1,0:T(8,128)} %shard_map.100) | data formatting | bytes 131072

commit v4 on v3

--- a/solution.py
+++ b/solution.py
@@ -172,9 +172,9 @@
     out, refs = refs[0], refs[1:]
     tables_vmem, refs = refs[:6], refs[6:]
     fh, fl, ih, il, twist, ends = tables_vmem
-    (slots, xin, turned, mid, land, stage, mid_ref, y_a, y_b, spec_ref, acc_ref, ends_f, ends_b, blocks, mid_o, land_o,
-     owned, square, near_sq, sums, tally,
-     insem, tabsem, s_a, r_a, s_b, r_b, l_a, l_b, s_ao, r_ao, s_bo, r_bo, s_n, r_n, s_q, r_q, l_o, far_sem) = refs
+    (slots, xin, turned, mid, land, stage, mid_ref, y_a, y_b, spec_ref, acc_ref, ends_f, ends_b, blocks, land_o,
+     owned, square, tally,
+     insem, tabsem, s_a, r_a, s_b, r_b, l_a, l_b, s_ao, r_ao, s_q, r_q, l_o, line_sem, far_sem) = refs
     z, x, c = place()
     ch = lax.axis_index("ch")
 
@@ -184,8 +184,13 @@
     def shift(kind, d, k, e):
         return at(e, d, k, 0) if kind == 0 else at(d, e, k, 0)
 
-    far = [(dz, dy) for dz in HOPS for dy in HOPS if (dz, dy) != (0, 0)]
+    others = [(dz, dx, k, dy) for dz in HOPS for dx in HOPS for k in (1, 0) for dy in HOPS]
+    others.remove((0, 0, 0, 0))
+    others.sort(key=lambda move: -sum(min(d, SIDE - d) for d in (move[0], move[1], move[3])))
     column = [(0, 0, 0, d) for d in HOPS[:3]]
+    line = [(d, 0, 0, 0) for d in HOPS[:3]]
+    plane = [(dz, dx, k) for dz in HOPS for dx in HOPS for k in (1, 0) if (dz, dx, k) != (0, 0, 0)]
+    plane.sort(key=lambda move: -min(move[0], SIDE - move[0]) - min(move[1], SIDE - move[1]))
     peers = {(0, d, k, 0) for d, k in MOVES} | {(d, 0, k, 0) for d, k in MOVES} | set(column)
     barrier = pltpu.get_barrier_semaphore()
     for peer in sorted(peers):
@@ -270,8 +275,8 @@
         for arr in range(2):
             for kind in range(2):
                 own_a(kind, kh, arr).start()
-    for peer in column:
-        pl.semaphore_signal(far_sem, inc=1, device_id=at(*peer), device_id_type=MESH)
+    for peer in line:
+        pl.semaphore_signal(line_sem, inc=1, device_id=at(*peer), device_id_type=MESH)
 
     def find(tile, carry):
         first, second = jnp.int32(0), jnp.int32(0)
@@ -295,6 +300,9 @@
                 send_b(kind, kh, arr, hop).start()
             own_b(kind, kh, arr).start()
 
+    pl.semaphore_wait(line_sem, len(line))
+    for peer in column:
+        pl.semaphore_signal(far_sem, inc=1, device_id=at(*peer), device_id_type=MESH)
     forward(0, 0)
     for copy in table_copies:
         copy.wait()
@@ -359,75 +367,40 @@
     dot = functools.partial(jnp.dot, preferred_element_type=F32)
     values = dot(ends_b[0], high) + (dot(ends_b[0], low) + dot(ends_b[1], high))
 
-    def send_n(move):
-        d, k = MOVES[move]
-        return pltpu.make_async_remote_copy(
-            src_ref=square,
-            dst_ref=near_sq.at[x * 2 + c],
-            send_sem=s_n.at[move],
-            recv_sem=r_n.at[move],
-            device_id=at(0, d, k, 0),
-            device_id_type=MESH,
-        )
-
     def send_q(k):
         return pltpu.make_async_remote_copy(
-            src_ref=sums,
-            dst_ref=tally.at[k],
-            send_sem=s_q.at[k],
-            recv_sem=r_q.at[k],
-            device_id=at(far[k][0], 0, 0, far[k][1]),
-            device_id_type=MESH,
-        )
+            src_ref=square, dst_ref=tally.at[k], send_sem=s_q, recv_sem=r_q, device_id=at(*others[k]), device_id_type=MESH
+        )
+
+    every_q = pltpu.make_async_remote_copy(
+        src_ref=tally, dst_ref=tally, send_sem=s_q, recv_sem=r_q, device_id=at(*others[0]), device_id_type=MESH
+    )
 
     def send_ao(move):
-        d, k = MOVES[move]
+        dz, dx, k = plane[move]
+        to = (((x + dx) % SIDE) * 2 + (c + k) % 2) * 4 + (z + dz) % SIDE
         return pltpu.make_async_remote_copy(
-            src_ref=blocks.at[pl.ds((((x + d) % SIDE) * 2 + (c + k) % 2) * 32, 32)],
-            dst_ref=mid_o.at[x * 2 + c],
+            src_ref=blocks.at[pl.ds(to * 8, 8)],
+            dst_ref=land_o.at[z * 8 + x * 2 + c],
             send_sem=s_ao.at[move],
             recv_sem=r_ao.at[move],
-            device_id=at(0, d, k, 0),
-            device_id_type=MESH,
-        )
-
-    def send_bo(hop):
-        return pltpu.make_async_remote_copy(
-            src_ref=mid_o.at[:, pl.ds(((z + HOPS[hop]) % SIDE) * 8, 8)],
-            dst_ref=land_o.at[pl.ds(z * 8, 8)],
-            send_sem=s_bo.at[hop],
-            recv_sem=r_bo.at[hop],
-            device_id=at(HOPS[hop], 0, 0, 0),
+            device_id=at(dz, dx, k, 0),
             device_id_type=MESH,
         )
 
     both = values[:, 0:128] * values[:, 0:128] + values[:, 128:256] * values[:, 128:256]
     own_square = jnp.sum(both, axis=0, keepdims=True)
     square[...] = own_square
-    for move in range(len(MOVES)):
-        send_n(move).start()
+    pl.semaphore_wait(far_sem, len(column))
+    for k in range(len(others)):
+        send_q(k).start()
     for kind in range(2):
         for half in range(2):
             blocks[pl.ds(2 * kind + half, 32, stride=8), :] = values[half * 32 : half * 32 + 32, kind * 128 : kind * 128 + 128]
-    for move in range(len(MOVES)):
+    for move in range(len(plane)):
         send_ao(move).start()
-    own_ao = pltpu.make_async_copy(blocks.at[pl.ds((x * 2 + c) * 32, 32)], mid_o.at[x * 2 + c], l_o.at[0])
+    own_ao = pltpu.make_async_copy(blocks.at[pl.ds(((x * 2 + c) * 4 + z) * 8, 8)], land_o.at[z * 8 + x * 2 + c], l_o)
     own_ao.start()
-    near_sq[x * 2 + c] = own_square
-    pl.semaphore_wait(far_sem, len(column))
-    own_ao.wait()
-    for move in range(len(MOVES)):
-        send_n(move).wait_recv()
-    line_sum = jnp.sum(near_sq[...], axis=0)
-    sums[...] = line_sum
-    for k in range(len(far)):
-        send_q(k).start()
-    for move in range(len(MOVES)):
-        send_ao(move).wait_recv()
-    for hop in range(3):
-        send_bo(hop).start()
-    own_bo = pltpu.make_async_copy(mid_o.at[:, pl.ds(z * 8, 8)], land_o.at[pl.ds(z * 8, 8)], l_o.at[1])
-    own_bo.start()
     for kh in range(2):
         for arr in range(2):
             for kind in range(2):
@@ -435,12 +408,9 @@
                     send_a(kind, kh, arr, move).wait_send()
                 for hop in range(3):
                     send_b(kind, kh, arr, hop).wait_send()
-    for move in range(len(MOVES)):
-        send_ao(move).wait_send()
-        send_n(move).wait_send()
-    own_bo.wait()
-    for hop in range(3):
-        send_bo(hop).wait_recv()
+    own_ao.wait()
+    for move in range(len(plane)):
+        send_ao(move).wait()
     rows = land_o.reshape(256, 128)
     for zz in range(4):
         for half in range(2):
@@ -448,13 +418,9 @@
             for cc in range(2):
                 to = half * 64 + 32 + 8 * zz + 4 * cc
                 owned[to : to + 4, :] = rows[pl.ds(zz * 64 + cc * 8 + 2 + half, 4, stride=16), :]
-    for hop in range(3):
-        send_bo(hop).wait_send()
-    for k in range(len(far)):
-        send_q(k).wait_send()
-    for k in range(len(far)):
-        send_q(k).wait_recv()
-    total = jnp.sum(line_sum + jnp.sum(tally[...], axis=0), axis=1, keepdims=True)
+    every_q.wait_send()
+    every_q.wait_recv()
+    total = jnp.sum(own_square + jnp.sum(tally[...], axis=0), axis=1, keepdims=True)
     total_entries = C // GROUP * POS // 2
     factor = target_ratio * math.sqrt(total_entries) / jnp.sqrt(total + epsilon)
     out[:, 0:128] = owned[0:64] * factor
@@ -469,7 +435,7 @@
     consts = [jnp.asarray(t) for t in tables()]
     return pl.pallas_call(
         fused_kernel,
-        out_shape=jax.ShapeDtypeStruct((64, 256), F32),
+        out_shape=pltpu.VMEM((64, 256), F32),
         in_specs=[smem, smem] + [hbm] * 8,
         out_specs=vmem,
         scratch_shapes=[pltpu.VMEM(t.shape, t.dtype) for t in consts]
@@ -488,16 +454,12 @@
             pltpu.VMEM((ROWS, 128), F32),
             pltpu.VMEM((2, ROWS, 128), BF16),
             pltpu.VMEM((256, 128), F32),
-            pltpu.VMEM((8, 32, 128), F32),
             pltpu.VMEM((32, 8, 128), F32),
             pltpu.VMEM((128, 128), F32),
             pltpu.VMEM((1, 128), F32),
-            pltpu.VMEM((8, 1, 128), F32),
-            pltpu.VMEM((1, 128), F32),
-            pltpu.VMEM((15, 1, 128), F32),
+            pltpu.VMEM((127, 1, 128), F32),
             dma((16,)), dma((6,)), dma((2, 2, 2, 7)), dma((2, 2, 2, 7)), dma((2, 2, 2, 3)), dma((2, 2, 2, 3)),
-            dma((2, 2, 2)), dma((2, 2, 2)), dma((7,)), dma((7,)), dma((3,)), dma((3,)), dma((7,)), dma((7,)),
-            dma((15,)), dma((15,)), dma((2,)), pltpu.SemaphoreType.REGULAR,
+            dma((2, 2, 2)), dma((2, 2, 2)), dma((31,)), dma((31,)), dma, dma, dma, pltpu.SemaphoreType.REGULAR, pltpu.SemaphoreType.REGULAR,
         ],
         compiler_params=pltpu.CompilerParams(collective_id=0, has_side_effects=True),
     )(tile_order, lag_order, inputs, out_grads, *consts)

time: 47.4 us -> 44.6 us (0.941)
  Pallas kernels: 45.6 us -> 43.9 us
  local copies, waits for them, and re-layouts: 1.47 us -> 0.63 us
    pallas_call x1, Pallas kernels: 45.6 us -> 43.9 us  [shards(): pl.pallas_call(fused_kernel, out_shape=pltpu.VMEM((64, 256), F32), in_spe...]
    unnamed x1, local copies, waits for them, and re-layouts: 1.47 us -> 0.63 us
where the time goes in v4:
time: 44.6 us; the launch traced here: 44.5 us
  Pallas kernels  43.9 us (98%)
  local copies, waits for them, and re-layouts  0.63 us (1%)
    pallas_call x1, Pallas kernels, shards(): pl.pallas_call(fused_kernel, out_shape=pltpu.VMEM((64, 256), F32), in_spe...  43.9 us

profile of v4, /device:TPU:1, one launch (start us, length us, event | category | flops | bytes accessed | tf_op | source)
XLA Modules:
  0.0 44.5 jit_solution(17092938447163869182)
XLA Ops:
  0.0 43.9 %shard_map.100 = f32[64,256]{1,0:T(8,128)S(1)} custom-call(s32[32]{0:T(128)} %tiles.1, s32[32]{0:T(128)} %lags.1, f32[256,1024]{1,0:T(8,128)} %u_ref.1, f32[256,1024]{1,0:T(8,128)} %g_ref.1, bf16[256,256]{1,0:T(8,128)(2,1)} %constant.12.clone.refs_0_, bf16[256,256]{1,0:T(8,128)(2,1)} %constant.13.clone.refs_1_, bf16[256,256]{1,0:T(8,128)(2,1)} %constant.14.clone.refs_2_, ...), custom_call_target="tpu_custom_call" | custom-call | tf_op jit(solution)/shard_map/pallas_call | solution.py:436
  43.9 0.6 %copy.12 = f32[64,256]{1,0:T(8,128)} copy(f32[64,256]{1,0:T(8,128)S(1)} %shard_map.100) | data formatting | bytes 131072

commit v5 on v4

--- a/solution.py
+++ b/solution.py
@@ -134,7 +134,7 @@
 
 
 def inner(y_ref, at, table):
-    return dot3((y_ref[0, at : at + 256], y_ref[1, at : at + 256]), table)
+    return dot3((y_ref[0], y_ref[1]), table)
 
 
 def channel_sums(rows):
@@ -154,7 +154,7 @@
 
 
 def multiply(grads, spec_ref, at, acc_ref):
-    for m in range(4):
+    for m in range(8):
         re, im = [], []
         for n in range(8):
             row = m * 64 + n * 8
@@ -167,14 +167,14 @@
         acc_ref[to : to + 8, 128:256] += channel_sums(im)
 
 
-def fused_kernel(tiles, lags, u_ref, g_ref, *refs):
+def fused_kernel(tiles_hbm, lags_hbm, u_ref, g_ref, *refs):
     tables_hbm, refs = refs[:6], refs[6:]
     out, refs = refs[0], refs[1:]
     tables_vmem, refs = refs[:6], refs[6:]
     fh, fl, ih, il, twist, ends = tables_vmem
-    (slots, xin, turned, mid, land, stage, mid_ref, y_a, y_b, spec_ref, acc_ref, ends_f, ends_b, blocks, land_o,
+    (tiles, lags, slots, xin, turned, mid, land, stage, mid_ref, y_a, y_b, spec_ref, acc_ref, ends_f, ends_b, blocks, land_o,
      owned, square, tally,
-     insem, tabsem, s_a, r_a, s_b, r_b, l_a, l_b, s_ao, r_ao, s_q, r_q, l_o, line_sem, far_sem) = refs
+     insem, ordsem, tabsem, s_a, r_a, s_b, r_b, l_a, l_b, s_ao, r_ao, s_q, r_q, l_o, line_sem, far_sem) = refs
     z, x, c = place()
     ch = lax.axis_index("ch")
 
@@ -208,6 +208,12 @@
                 )
                 copy.start()
                 incoming.append((copy, step, kind, a, arr))
+    order_copies = [
+        pltpu.make_async_copy(tiles_hbm, tiles, ordsem.at[0]),
+        pltpu.make_async_copy(lags_hbm, lags, ordsem.at[1]),
+    ]
+    for copy in order_copies:
+        copy.start()
     table_copies = [pltpu.make_async_copy(h, v, tabsem.at[n]) for n, (h, v) in enumerate(zip(tables_hbm, tables_vmem))]
     for copy in table_copies:
         copy.start()
@@ -278,6 +284,9 @@
     for peer in line:
         pl.semaphore_signal(line_sem, inc=1, device_id=at(*peer), device_id_type=MESH)
 
+    for copy in order_copies:
+        copy.wait()
+
     def find(tile, carry):
         first, second = jnp.int32(0), jnp.int32(0)
         for s in range(32):
@@ -328,7 +337,7 @@
         return lambda tile, half: stage[slots[kind, tile], :, half * 128 : half * 128 + 128]
 
     def spectra(kind, y_ref, part):
-        spec_ref[kind, part * 256 : part * 256 + 256] = inner(y_ref, part * 256, inner_table)
+        spec_ref[kind] = inner(y_ref, part * 256, inner_table)
 
     def products(kind, y_ref, part):
         multiply(inner(y_ref, part * 256, inner_table), spec_ref.at[kind], part * 256, acc_ref.at[kind])
@@ -339,20 +348,15 @@
         load = take(1, kh, 0)
         spectra(0, y_a, 0)
         outer_first(load, mid_ref)
-        spectra(0, y_a, 1)
         outer_second(twist, mid_ref, y_b)
-        load = take(0, kh, 1)
         spectra(1, y_b, 0)
-        outer_first(load, mid_ref)
-        spectra(1, y_b, 1)
+        outer_first(take(0, kh, 1), mid_ref)
         outer_second(twist, mid_ref, y_a)
         load = take(1, kh, 1)
         products(0, y_a, 0)
         outer_first(load, mid_ref)
-        products(0, y_a, 1)
         outer_second(twist, mid_ref, y_b)
         products(1, y_b, 0)
-        products(1, y_b, 1)
         return carry
 
     lax.fori_loop(0, 2, chunk, 0)
@@ -429,17 +433,18 @@
 
 def shards(inputs, out_grads, tile_order, lag_order):
     vmem = pl.BlockSpec(memory_space=pltpu.VMEM)
-    smem = pl.BlockSpec(memory_space=pltpu.SMEM)
     hbm = pl.BlockSpec(memory_space=pl.ANY)
     dma = pltpu.SemaphoreType.DMA
     consts = [jnp.asarray(t) for t in tables()]
     return pl.pallas_call(
         fused_kernel,
         out_shape=pltpu.VMEM((64, 256), F32),
-        in_specs=[smem, smem] + [hbm] * 8,
+        in_specs=[hbm] * 10,
         out_specs=vmem,
         scratch_shapes=[pltpu.VMEM(t.shape, t.dtype) for t in consts]
         + [
+            pltpu.SMEM((32,), jnp.int32),
+            pltpu.SMEM((32,), jnp.int32),
             pltpu.SMEM((2, 32), jnp.int32),
             pltpu.VMEM((16, 256, 128), F32),
             pltpu.VMEM((2, 4, 2, 4, 2, 2, 8, 256), F32),
@@ -458,7 +463,7 @@
             pltpu.VMEM((128, 128), F32),
             pltpu.VMEM((1, 128), F32),
             pltpu.VMEM((127, 1, 128), F32),
-            dma((16,)), dma((6,)), dma((2, 2, 2, 7)), dma((2, 2, 2, 7)), dma((2, 2, 2, 3)), dma((2, 2, 2, 3)),
+            dma((16,)), dma((2,)), dma((6,)), dma((2, 2, 2, 7)), dma((2, 2, 2, 7)), dma((2, 2, 2, 3)), dma((2, 2, 2, 3)),
             dma((2, 2, 2)), dma((2, 2, 2)), dma((31,)), dma((31,)), dma, dma, dma, pltpu.SemaphoreType.REGULAR, pltpu.SemaphoreType.REGULAR,
         ],
         compiler_params=pltpu.CompilerParams(collective_id=0, has_side_effects=True),

time: 44.6 us -> 43.6 us (0.978)
  Pallas kernels: 43.9 us -> 42.8 us
    pallas_call x1, Pallas kernels: 43.9 us -> 42.8 us  [shards(): pl.pallas_call(fused_kernel, out_shape=pltpu.VMEM((64, 256), F32), in_spe...]
where the time goes in v5:
time: 43.6 us; the launch traced here: 43.5 us
  Pallas kernels  42.8 us (98%)
  local copies, waits for them, and re-layouts  0.63 us (1%)
    pallas_call x1, Pallas kernels, shards(): pl.pallas_call(fused_kernel, out_shape=pltpu.VMEM((64, 256), F32), in_spe...  42.8 us

profile of v5, /device:TPU:1, one launch (start us, length us, event | category | flops | bytes accessed | tf_op | source)
XLA Modules:
  0.0 43.5 jit_solution(11950122573942828083)
XLA Ops:
  0.0 42.8 %shard_map.100 = f32[64,256]{1,0:T(8,128)S(1)} custom-call(s32[32]{0:T(128)} %tiles_hbm.1, s32[32]{0:T(128)} %lags_hbm.1, f32[256,1024]{1,0:T(8,128)} %u_ref.1, f32[256,1024]{1,0:T(8,128)} %g_ref.1, bf16[256,256]{1,0:T(8,128)(2,1)} %constant.12.clone.refs_0_, bf16[256,256]{1,0:T(8,128)(2,1)} %constant.13.clone.refs_1_, ...), custom_call_target="tpu_custom_call" | custom-call | tf_op jit(solution)/shard_map/pallas_call | solution.py:439
  42.9 0.6 %copy.12 = f32[64,256]{1,0:T(8,128)} copy(f32[64,256]{1,0:T(8,128)S(1)} %shard_map.100) | data formatting | bytes 131072

commit v6 on v5

--- a/solution.py
+++ b/solution.py
@@ -19,6 +19,8 @@
 SIDE = 4
 POS = 16384
 ROWS = 64
+PARTS = 4
+PART = ROWS * 8 // PARTS
 HOPS = (2, 1, 3, 0)
 MOVES = tuple((d, k) for d in HOPS for k in (0, 1) if (d, k) != (0, 0))
 
@@ -115,8 +117,8 @@
                 mid_ref[m, 2 * q2 + half, 1] = out[m][1]
 
 
-def outer_second(twist_ref, mid_ref, y_ref):
-    for m in range(8):
+def outer_second(twist_ref, mid_ref, y_ref, start=0, stop=8):
+    for m in range(start, stop):
         z = []
         for q in range(8):
             re, im = mid_ref[m, q, 0], mid_ref[m, q, 1]
@@ -133,8 +135,8 @@
                     y_ref[k, (8 * m + n) * 8 : (8 * m + n) * 8 + 16, part * 128 : part * 128 + 128] = pair[k]
 
 
-def inner(y_ref, at, table):
-    return dot3((y_ref[0], y_ref[1]), table)
+def inner(y_ref, at, count, table):
+    return dot3((y_ref[0, at : at + count], y_ref[1, at : at + count]), table)
 
 
 def channel_sums(rows):
@@ -154,7 +156,7 @@
 
 
 def multiply(grads, spec_ref, at, acc_ref):
-    for m in range(8):
+    for m in range(grads.shape[0] // 64):
         re, im = [], []
         for n in range(8):
             row = m * 64 + n * 8
@@ -172,7 +174,7 @@
     out, refs = refs[0], refs[1:]
     tables_vmem, refs = refs[:6], refs[6:]
     fh, fl, ih, il, twist, ends = tables_vmem
-    (tiles, lags, slots, xin, turned, mid, land, stage, mid_ref, y_a, y_b, spec_ref, acc_ref, ends_f, ends_b, blocks, land_o,
+    (tiles, lags, slots, xin, turned, mid, land, stage, stage_b, mid_ref, mid_b, y_a, y_b, spec_ref, acc_ref, ends_f, ends_b, blocks, land_o,
      owned, square, tally,
      insem, ordsem, tabsem, s_a, r_a, s_b, r_b, l_a, l_b, s_ao, r_ao, s_q, r_q, l_o, line_sem, far_sem) = refs
     z, x, c = place()
@@ -329,34 +331,38 @@
     forward(1, 1)
     inner_table = (fh[...], fl[...])
 
-    def take(kind, kh, arr):
+    def take(kind, kh, arr, held=stage):
         own_b(kind, kh, arr).wait()
         for hop in range(3):
             send_b(kind, kh, arr, hop).wait_recv()
-        stage[...] = land[kind, kh, arr]
-        return lambda tile, half: stage[slots[kind, tile], :, half * 128 : half * 128 + 128]
-
-    def spectra(kind, y_ref, part):
-        spec_ref[kind] = inner(y_ref, part * 256, inner_table)
+        held[...] = land[kind, kh, arr]
+        return lambda tile, half: held[slots[kind, tile], :, half * 128 : half * 128 + 128]
+
+    def spectra(kind, y_ref):
+        spec_ref[kind] = inner(y_ref, 0, ROWS * 8, inner_table)
 
     def products(kind, y_ref, part):
-        multiply(inner(y_ref, part * 256, inner_table), spec_ref.at[kind], part * 256, acc_ref.at[kind])
+        grads = inner(y_ref, part * PART, PART, inner_table)
+        multiply(grads, spec_ref.at[kind], part * PART, acc_ref.at[kind])
 
     def chunk(kh, carry):
         outer_first(take(0, kh, 0), mid_ref)
         outer_second(twist, mid_ref, y_a)
         load = take(1, kh, 0)
-        spectra(0, y_a, 0)
+        spectra(0, y_a)
         outer_first(load, mid_ref)
         outer_second(twist, mid_ref, y_b)
-        spectra(1, y_b, 0)
-        outer_first(take(0, kh, 1), mid_ref)
-        outer_second(twist, mid_ref, y_a)
-        load = take(1, kh, 1)
-        products(0, y_a, 0)
+        spectra(1, y_b)
+        load = take(0, kh, 1)
+        later = take(1, kh, 1, stage_b)
         outer_first(load, mid_ref)
-        outer_second(twist, mid_ref, y_b)
-        products(1, y_b, 0)
+        for part in range(PARTS):
+            outer_second(twist, mid_ref, y_a, part * 8 // PARTS, (part + 1) * 8 // PARTS)
+            products(0, y_a, part)
+        outer_first(later, mid_b)
+        for part in range(PARTS):
+            outer_second(twist, mid_b, y_b, part * 8 // PARTS, (part + 1) * 8 // PARTS)
+            products(1, y_b, part)
         return carry
 
     lax.fori_loop(0, 2, chunk, 0)
@@ -451,6 +457,8 @@
             pltpu.VMEM((2, 2, 2, 4, 8, 8, 256), F32),
             pltpu.VMEM((2, 2, 2, 32, 8, 256), F32),
             pltpu.VMEM((32, 8, 256), F32),
+            pltpu.VMEM((32, 8, 256), F32),
+            pltpu.VMEM((8, 8, 2, 8, 128), F32),
             pltpu.VMEM((8, 8, 2, 8, 128), F32),
             pltpu.VMEM((2, ROWS * 8, 256), BF16),
             pltpu.VMEM((2, ROWS * 8, 256), BF16),

time: 43.6 us -> 43.7 us (level)
  no operation moved by 1% of the time
where the time goes in v6:
time: 43.7 us; the launch traced here: 43.6 us
  Pallas kernels  42.9 us (98%)
  local copies, waits for them, and re-layouts  0.63 us (1%)
    pallas_call x1, Pallas kernels, shards(): pl.pallas_call(fused_kernel, out_shape=pltpu.VMEM((64, 256), F32), in_spe...  42.9 us

profile of v6, /device:TPU:1, one launch (start us, length us, event | category | flops | bytes accessed | tf_op | source)
XLA Modules:
  0.0 43.6 jit_solution(13367267276098457972)
XLA Ops:
  0.0 42.9 %shard_map.100 = f32[64,256]{1,0:T(8,128)S(1)} custom-call(s32[32]{0:T(128)} %tiles_hbm.1, s32[32]{0:T(128)} %lags_hbm.1, f32[256,1024]{1,0:T(8,128)} %u_ref.1, f32[256,1024]{1,0:T(8,128)} %g_ref.1, bf16[256,256]{1,0:T(8,128)(2,1)} %constant.12.clone.refs_0_, bf16[256,256]{1,0:T(8,128)(2,1)} %constant.13.clone.refs_1_, ...), custom_call_target="tpu_custom_call" | custom-call | tf_op jit(solution)/shard_map/pallas_call | solution.py:445
  42.9 0.6 %copy.12 = f32[64,256]{1,0:T(8,128)} copy(f32[64,256]{1,0:T(8,128)S(1)} %shard_map.100) | data formatting | bytes 131072
